TPU v7x, 512 devices: a whole 4x8x8 slice. The times are simulated.
512 devices in a mesh: ctx: 64 (over z, x, core), head: 8 (over y).
Axes of the slice: x: 4, y: 8, z: 8, core: 2. Of those that a mesh axis runs over, the one named last changes fastest.
Arguments:
- queries: bfloat16 [16384, 4096], P(('ctx', 'head')), may hold values from -6 to 6
- key_rows: bfloat16 [16384, 4096], P(('ctx', 'head')), may hold values from -6 to 6
- value_rows: bfloat16 [16384, 4096], P(('ctx', 'head')), may hold values from -6 to 6
- grad_out: bfloat16 [16384, 4096], P(('ctx', 'head')), may hold values from -6 to 6
Outputs:
- grad_query: bfloat16 [16384, 4096], P(('ctx', 'head'))
- grad_key: bfloat16 [16384, 4096], P(('ctx', 'head'))
- grad_value: bfloat16 [16384, 4096], P(('ctx', 'head'))
All inputs are finite; a program needn't handle non-finite values.
Results may differ from a plain program's by a relative error of at most 0.0021.
Values may be sent and summed in bfloat16 or wider, within the bound.
A program may use at most 128 MiB of HBM per device.

v0:
```python
import jax
import jax.numpy as jnp
from jax import lax
from jax.sharding import PartitionSpec as P

HEAD_DIM = 128
GROUP = 128


def entering(part, axis, combine, identity, reverse):
    count = lax.axis_size(axis)
    place = lax.axis_index(axis)
    ahead = count - 1 - place if reverse else place
    gathered = lax.all_gather(part, axis)
    state = jnp.zeros_like(part) + jnp.asarray(identity, part.dtype)

    def one(turn, state):
        source = count - 1 - turn if reverse else turn
        return combine(state, lax.dynamic_index_in_dim(gathered, source, 0, False))

    return lax.fori_loop(0, ahead, one, state)


def add_states(earlier, later):
    return jax.tree.map(jnp.add, earlier, later)


def per_device(queries, key_rows, value_rows, grad_out):
    q_all, k_all, v_all, d_all = (
        lax.all_to_all(queries, "head", split_axis=1, concat_axis=0, tiled=True),
        lax.all_to_all(key_rows, "head", split_axis=1, concat_axis=0, tiled=True),
        lax.all_to_all(value_rows, "head", split_axis=1, concat_axis=0, tiled=True),
        lax.all_to_all(grad_out, "head", split_axis=1, concat_axis=0, tiled=True),
    )
    rows_here = q_all.shape[0]
    heads_here = q_all.shape[1] // HEAD_DIM
    scale = (HEAD_DIM * rows_here * lax.axis_size("ctx")) ** (-0.5)
    highest = lax.Precision.HIGHEST
    block = GROUP
    nblocks = rows_here // block
    shape_four = (nblocks, block, heads_here, HEAD_DIM)
    q_four = q_all.reshape(shape_four)
    k_four = k_all.reshape(shape_four)
    v_four = v_all.reshape(shape_four)
    d_four = d_all.reshape(shape_four)
    kv_blocks = jnp.einsum("ntha,nthb->nhab", v_four, k_four, preferred_element_type=jnp.float32)
    g_blocks = jnp.einsum("ntha,nthb->nhab", d_four, q_four, preferred_element_type=jnp.float32)
    kv_local = jnp.sum(kv_blocks, axis=0)
    g_local = jnp.sum(g_blocks, axis=0)
    zeros_state = jnp.zeros_like(kv_local)
    kv_before = entering(kv_local, "ctx", add_states, zeros_state, False)
    g_after = entering(g_local, "ctx", add_states, zeros_state, True)
    row_ids = lax.broadcasted_iota(jnp.int32, (nblocks, nblocks), 0)
    col_ids = lax.broadcasted_iota(jnp.int32, (nblocks, nblocks), 1)
    strict_lower = (col_ids < row_ids).astype(jnp.float32)
    strict_upper = (col_ids > row_ids).astype(jnp.float32)
    kv_in = kv_before[None] + jnp.einsum(
        "mn,nhab->mhab", strict_lower, kv_blocks, precision=highest
    )
    g_in = g_after[None] + jnp.einsum("mn,nhab->mhab", strict_upper, g_blocks, precision=highest)
    later = lax.broadcasted_iota(jnp.int32, (block, block), 0)
    earlier = lax.broadcasted_iota(jnp.int32, (block, block), 1)
    causal = (later >= earlier).astype(jnp.float32)
    scores = (
        jnp.einsum("nthd,nshd->nhts", q_four, k_four, preferred_element_type=jnp.float32)
        * (scale * causal)
    ).astype(jnp.bfloat16)
    dscores = (
        jnp.einsum("nthd,nshd->nhts", d_four, v_four, preferred_element_type=jnp.float32) * causal
    ).astype(jnp.bfloat16)
    k_float = k_four.astype(jnp.float32)
    v_float = v_four.astype(jnp.float32)
    d_float = d_four.astype(jnp.float32)
    grad_q = scale * (
        jnp.einsum("nhts,nshd->nthd", dscores, k_four, preferred_element_type=jnp.float32)
        + jnp.einsum("ntha,nhab->nthb", d_float, kv_in, precision=highest)
    )
    grad_k = scale * (
        jnp.einsum("nhts,nthd->nshd", dscores, q_four, preferred_element_type=jnp.float32)
        + jnp.einsum("ntha,nhab->nthb", v_float, g_in, precision=highest)
    )
    grad_v = jnp.einsum(
        "nhts,nthd->nshd", scores, d_four, preferred_element_type=jnp.float32
    ) + scale * jnp.einsum("nthb,nhab->ntha", k_float, g_in, precision=highest)
    flat_shape = (rows_here, heads_here * HEAD_DIM)
    grad_q = grad_q.reshape(flat_shape).astype(jnp.bfloat16)
    grad_k = grad_k.reshape(flat_shape).astype(jnp.bfloat16)
    grad_v = grad_v.reshape(flat_shape).astype(jnp.bfloat16)
    result_q, result_k, result_v = (
        lax.all_to_all(grad_q, "head", split_axis=0, concat_axis=1, tiled=True),
        lax.all_to_all(grad_k, "head", split_axis=0, concat_axis=1, tiled=True),
        lax.all_to_all(grad_v, "head", split_axis=0, concat_axis=1, tiled=True),
    )
    return (result_q, result_k, result_v)


def solution(mesh):
    placed = (
        P(("ctx", "head"), None),
        P(("ctx", "head"), None),
        P(("ctx", "head"), None),
        P(("ctx", "head"), None),
    )
    return jax.shard_map(
        per_device,
        mesh=mesh,
        in_specs=placed,
        out_specs=(P(("ctx", "head"), None), P(("ctx", "head"), None), P(("ctx", "head"), None)),
        check_vma=False,
    )
```

profile of v0, /device:TPU:1, one launch (start us, length us, event | category | flops | bytes accessed | tf_op | source)
XLA Modules:
  0.0 359.6 jit_solution(15436191070867559505)
XLA Ops:
  7.2 1.7 copy.181
  8.8 7.7 %all-to-all-start.2 = ((bf16[32,8,512]{2,0,1:T(8,128)(2,1)}), bf16[32,8,512]{2,0,1:T(8,128)(2,1)S(1)}, u32[]{:S(2)}, u32[]{:S(2)}) async-start(bf16[32,8,512]{2,0,1:T(8,128)(2,1)} %bitcast.72), calls=%async_computation.2 | async-start | bytes 524288 | tf_op jit(solution)/shard_map/all_to_all | solution.py:31
  16.5 1.7 copy.182
  18.2 7.7 %all-to-all-done.2 = bf16[32,8,512]{2,0,1:T(8,128)(2,1)S(1)} async-done(((bf16[32,8,512]{2,0,1:T(8,128)(2,1)}), bf16[32,8,512]{2,0,1:T(8,128)(2,1)S(1)}, u32[]{:S(2)}, u32[]{:S(2)}) %all-to-all-start.2) | async-done | bytes 262176 | tf_op jit(solution)/shard_map/all_to_all | solution.py:31
  25.9 3.4 all-to-all-start.1
  29.4 9.3 %all-to-all-done.1 = bf16[32,8,512]{2,0,1:T(8,128)(2,1)S(1)} async-done(((bf16[32,8,512]{2,0,1:T(8,128)(2,1)}), bf16[32,8,512]{2,0,1:T(8,128)(2,1)S(1)}, u32[]{:S(2)}, u32[]{:S(2)}) %all-to-all-start.1) | async-done | bytes 262176 | tf_op jit(solution)/shard_map/all_to_all | solution.py:32
  39.8 1.7 copy.183
  41.5 3.4 all-to-all-start
  44.9 1.7 copy.180
  46.6 7.7 %all-to-all-done = bf16[32,8,512]{2,0,1:T(8,128)(2,1)S(1)} async-done(((bf16[32,8,512]{2,0,1:T(8,128)(2,1)}), bf16[32,8,512]{2,0,1:T(8,128)(2,1)S(1)}, u32[]{:S(2)}, u32[]{:S(2)}) %all-to-all-start) | async-done | bytes 262176 | tf_op jit(solution)/shard_map/all_to_all | solution.py:33
  54.2 3.4 all-to-all-start.4
  57.8 9.1 %all-to-all-done.4 = bf16[32,8,512]{2,0,1:T(8,128)(2,1)S(1)} async-done(((bf16[32,8,512]{2,0,1:T(8,128)(2,1)}), bf16[32,8,512]{2,0,1:T(8,128)(2,1)S(1)}, u32[]{:S(2)}, u32[]{:S(2)}) %all-to-all-start.4) | async-done | bytes 262176 | tf_op jit(solution)/shard_map/all_to_all | solution.py:30
  68.3 81.1 %all-gather.5.cloned.1.call-done = f32[256,128,128]{2,1,0:T(8,128)} async-done(((f32[4,128,128]{2,1,0:T(8,128)}), f32[256,128,128]{2,1,0:T(8,128)}) %all-gather.5.cloned.1.call-update) | async-done | bytes 16777232 | tf_op jit(solution)/shard_map/all_gather | solution.py:14
  149.5 1.0 while.22
  149.5 1.0 bitcast_add_fusion.4
  150.5 1.4 convolution_add_fusion.1
  153.6 6.5 %all-to-all-start.3 = ((bf16[8,32,512]{2,1,0:T(8,128)(2,1)}), bf16[8,32,512]{2,1,0:T(8,128)(2,1)S(1)}, u32[]{:S(2)}, u32[]{:S(2)}) async-start(bf16[8,32,512]{2,1,0:T(8,128)(2,1)} %convert_element_type.42), calls=%async_computation.3 | async-start | bytes 524288 | tf_op jit(solution)/shard_map/all_to_all | solution.py:90
  160.0 95.8 %all-gather.7.cloned.1.call-done = f32[256,128,128]{2,1,0:T(8,128)} async-done(((f32[4,128,128]{2,1,0:T(8,128)}), f32[256,128,128]{2,1,0:T(8,128)}) %all-gather.7.cloned.1.call-update) | async-done | bytes 16777232 | tf_op jit(solution)/shard_map/all_gather | solution.py:14
  255.9 64.1 %while.23 = (s32[]{:T(128)}, f32[4,128,128]{2,1,0:T(8,128)S(1)}, s32[]{:T(128)}, f32[64,4,128,128]{3,2,1,0:T(8,128)}, s32[]{:T(128)}, /*index=5*/s32[]{:T(128)}, s32[]{:T(128)}, s32[]{:T(128)}) while((s32[]{:T(128)}, f32[4,128,128]{2,1,0:T(8,128)S(1)}, s32[]{:T(128)}, f32[64,4,128,128]{3,2,1,0:T(8,128)}, s32[]{:T(128)}, /*index=5*/s32[]{:T(128)}, ...), condition=%wide.region_5.6_spmd, body=%wide.region_4.5_spmd.sunk | while | flops 65542 | bytes 786575 | solution.py:21
  255.9 1.0 bitcast_add_fusion.5
  256.9 1.0 bitcast_add_fusion.5
  258.0 1.0 bitcast_add_fusion.5
  259.0 1.0 bitcast_add_fusion.5
  260.0 1.0 bitcast_add_fusion.5
  261.1 1.0 bitcast_add_fusion.5
  262.1 1.0 bitcast_add_fusion.5
  263.1 1.0 bitcast_add_fusion.5
  264.2 1.0 bitcast_add_fusion.5
  265.2 1.0 bitcast_add_fusion.5
  266.2 1.0 bitcast_add_fusion.5
  267.3 1.0 bitcast_add_fusion.5
  268.3 1.0 bitcast_add_fusion.5
  269.3 1.0 bitcast_add_fusion.5
  270.4 1.0 bitcast_add_fusion.5
  271.4 1.0 bitcast_add_fusion.5
  272.4 1.0 bitcast_add_fusion.5
  273.5 1.0 bitcast_add_fusion.5
  274.5 1.0 bitcast_add_fusion.5
  275.5 1.0 bitcast_add_fusion.5
  276.6 1.0 bitcast_add_fusion.5
  277.6 1.0 bitcast_add_fusion.5
  278.6 1.0 bitcast_add_fusion.5
  279.7 1.0 bitcast_add_fusion.5
  280.7 1.0 bitcast_add_fusion.5
  281.7 1.0 bitcast_add_fusion.5
  282.8 1.0 bitcast_add_fusion.5
  283.8 1.0 bitcast_add_fusion.5
  284.8 1.0 bitcast_add_fusion.5
  285.9 1.0 bitcast_add_fusion.5
  286.9 1.0 bitcast_add_fusion.5
  294.1 1.0 bitcast_add_fusion.5
  295.2 1.0 bitcast_add_fusion.5
  296.2 1.0 bitcast_add_fusion.5
  304.5 1.0 bitcast_add_fusion.5
  305.5 1.0 bitcast_add_fusion.5
  306.5 1.0 bitcast_add_fusion.5
  313.8 1.0 bitcast_add_fusion.5
  314.8 1.0 bitcast_add_fusion.5
  315.8 1.0 bitcast_add_fusion.5
  319.9 1.4 convolution_add_fusion
  323.0 6.5 %all-to-all-start.5 = ((bf16[8,32,512]{2,1,0:T(8,128)(2,1)}), bf16[8,32,512]{2,1,0:T(8,128)(2,1)S(1)}, u32[]{:S(2)}, u32[]{:S(2)}) async-start(bf16[8,32,512]{2,1,0:T(8,128)(2,1)} %convert_element_type.44), calls=%async_computation.5 | async-start | bytes 524288 | tf_op jit(solution)/shard_map/all_to_all | solution.py:91
  331.7 7.6 %all-to-all-done.5 = bf16[8,32,512]{2,1,0:T(8,128)(2,1)S(1)} async-done(((bf16[8,32,512]{2,1,0:T(8,128)(2,1)}), bf16[8,32,512]{2,1,0:T(8,128)(2,1)S(1)}, u32[]{:S(2)}, u32[]{:S(2)}) %all-to-all-start.5) | async-done | bytes 262176 | tf_op jit(solution)/shard_map/all_to_all | solution.py:91
  339.4 3.4 all-to-all-start.6
  344.2 7.9 %all-to-all-done.6 = bf16[8,32,512]{2,1,0:T(8,128)(2,1)S(1)} async-done(((bf16[8,32,512]{2,1,0:T(8,128)(2,1)}), bf16[8,32,512]{2,1,0:T(8,128)(2,1)S(1)}, u32[]{:S(2)}, u32[]{:S(2)}) %all-to-all-start.6) | async-done | bytes 262176 | tf_op jit(solution)/shard_map/all_to_all | solution.py:92
  (53 shorter events, 32.6 us)
Async XLA Ops:
  8.8 17.1 %all-to-all-start.2 = ((bf16[32,8,512]{2,0,1:T(8,128)(2,1)}), bf16[32,8,512]{2,0,1:T(8,128)(2,1)S(1)}, u32[]{:S(2)}, u32[]{:S(2)}) async-start(bf16[32,8,512]{2,0,1:T(8,128)(2,1)} %bitcast.72), calls=%async_computation.2 | async-start | bytes 524288 | tf_op jit(solution)/shard_map/all_to_all | solution.py:31
  25.9 12.8 %all-to-all-start.1 = ((bf16[32,8,512]{2,0,1:T(8,128)(2,1)}), bf16[32,8,512]{2,0,1:T(8,128)(2,1)S(1)}, u32[]{:S(2)}, u32[]{:S(2)}) async-start(bf16[32,8,512]{2,0,1:T(8,128)(2,1)} %bitcast.73), calls=%async_computation.1 | async-start | bytes 524288 | tf_op jit(solution)/shard_map/all_to_all | solution.py:32
  29.3 120.1 %all-gather.5.cloned.1.call-start = ((), (), s32[]{:S(2)}) async-start(), calls=%async_computation.7 | async-start | bytes 17039360 | tf_op jit(solution)/shard_map/all_gather | solution.py:14
  41.5 12.8 %all-to-all-start = ((bf16[32,8,512]{2,0,1:T(8,128)(2,1)}), bf16[32,8,512]{2,0,1:T(8,128)(2,1)S(1)}, u32[]{:S(2)}, u32[]{:S(2)}) async-start(bf16[32,8,512]{2,0,1:T(8,128)(2,1)} %bitcast.74), calls=%async_computation | async-start | bytes 524288 | tf_op jit(solution)/shard_map/all_to_all | solution.py:33
  54.2 12.7 %all-to-all-start.4 = ((bf16[32,8,512]{2,0,1:T(8,128)(2,1)}), bf16[32,8,512]{2,0,1:T(8,128)(2,1)S(1)}, u32[]{:S(2)}, u32[]{:S(2)}) async-start(bf16[32,8,512]{2,0,1:T(8,128)(2,1)} %bitcast.71), calls=%async_computation.4 | async-start | bytes 524288 | tf_op jit(solution)/shard_map/all_to_all | solution.py:30
  57.7 198.2 %all-gather.7.cloned.1.call-start = ((), (), s32[]{:S(2)}) async-start(), calls=%async_computation.8 | async-start | bytes 17039360 | tf_op jit(solution)/shard_map/all_gather | solution.py:14
  153.6 169.5 %all-to-all-start.3 = ((bf16[8,32,512]{2,1,0:T(8,128)(2,1)}), bf16[8,32,512]{2,1,0:T(8,128)(2,1)S(1)}, u32[]{:S(2)}, u32[]{:S(2)}) async-start(bf16[8,32,512]{2,1,0:T(8,128)(2,1)} %convert_element_type.42), calls=%async_computation.3 | async-start | bytes 524288 | tf_op jit(solution)/shard_map/all_to_all | solution.py:90
  323.0 16.3 %all-to-all-start.5 = ((bf16[8,32,512]{2,1,0:T(8,128)(2,1)}), bf16[8,32,512]{2,1,0:T(8,128)(2,1)S(1)}, u32[]{:S(2)}, u32[]{:S(2)}) async-start(bf16[8,32,512]{2,1,0:T(8,128)(2,1)} %convert_element_type.44), calls=%async_computation.5 | async-start | bytes 524288 | tf_op jit(solution)/shard_map/all_to_all | solution.py:91
  339.4 12.7 %all-to-all-start.6 = ((bf16[8,32,512]{2,1,0:T(8,128)(2,1)}), bf16[8,32,512]{2,1,0:T(8,128)(2,1)S(1)}, u32[]{:S(2)}, u32[]{:S(2)}) async-start(bf16[8,32,512]{2,1,0:T(8,128)(2,1)} %convert_element_type.47), calls=%async_computation.6 | async-start | bytes 524288 | tf_op jit(solution)/shard_map/all_to_all | solution.py:92
Sparse Core Ops, SparseCore 0:
  39.9 109.5 all-gather.4
  153.4 102.4 all-gather.6
where the time goes:
time: 364 us; the launch traced here: 360 us
  waiting for transfers between devices  226 us (62%)
  other arithmetic  63.7 us (18%)
  starting transfers between devices  34.3 us (9%)
  between operations  14.2 us (4%)
  local copies, waits for them, and re-layouts  12.2 us (3%)
  matrix products  7.47 us (2%)
    all_gather x2, waiting for transfers between devices, entering(): gathered = lax.all_gather(part, axis)  177 us
    add x63, other arithmetic, add_states(): return jax.tree.map(jnp.add, earlier, later)  63.7 us
    all_to_all x1, waiting for transfers between devices, per_device(): lax.all_to_all(value_rows, 'head', split_axis=1, concat_axis=0, tiled=True)  9.28 us
    all_to_all x1, waiting for transfers between devices, per_device(): lax.all_to_all(queries, 'head', split_axis=1, concat_axis=0, tiled=True)  9.13 us
    all_to_all x1, waiting for transfers between devices, per_device(): lax.all_to_all(grad_v, 'head', split_axis=0, concat_axis=1, tiled=True)  7.85 us
    all_to_all x1, waiting for transfers between devices, per_device(): lax.all_to_all(key_rows, 'head', split_axis=1, concat_axis=0, tiled=True)  7.73 us
    all_to_all x1, waiting for transfers between devices, per_device(): lax.all_to_all(grad_out, 'head', split_axis=1, concat_axis=0, tiled=True)  7.67 us
    all_to_all x1, starting transfers between devices, per_device(): lax.all_to_all(key_rows, 'head', split_axis=1, concat_axis=0, tiled=True)  7.65 us
  transfers between devices with their start and end apart: 9, of which 8 were waited for; matrix products, arithmetic and copies ran while one was open for 22% of the time, Pallas kernels for 0%

commit v1 on v0

--- a/solution.py
+++ b/solution.py
@@ -7,30 +7,29 @@
 GROUP = 128
 
 
-def entering(part, axis, combine, identity, reverse):
+def exclusive_scans(forward_part, backward_part, axis):
     count = lax.axis_size(axis)
-    place = lax.axis_index(axis)
-    ahead = count - 1 - place if reverse else place
-    gathered = lax.all_gather(part, axis)
-    state = jnp.zeros_like(part) + jnp.asarray(identity, part.dtype)
-
-    def one(turn, state):
-        source = count - 1 - turn if reverse else turn
-        return combine(state, lax.dynamic_index_in_dim(gathered, source, 0, False))
-
-    return lax.fori_loop(0, ahead, one, state)
-
-
-def add_states(earlier, later):
-    return jax.tree.map(jnp.add, earlier, later)
+    fwd_total, fwd_excl = forward_part, jnp.zeros_like(forward_part)
+    bwd_total, bwd_excl = backward_part, jnp.zeros_like(backward_part)
+    shift = 1
+    while shift < count:
+        to_right = [(i, i + shift) for i in range(count - shift)]
+        to_left = [(i + shift, i) for i in range(count - shift)]
+        got_fwd = lax.ppermute(fwd_total, axis, to_right)
+        got_bwd = lax.ppermute(bwd_total, axis, to_left)
+        fwd_excl = fwd_excl + got_fwd
+        bwd_excl = bwd_excl + got_bwd
+        if shift * 2 < count:
+            fwd_total = fwd_total + got_fwd
+            bwd_total = bwd_total + got_bwd
+        shift *= 2
+    return fwd_excl, bwd_excl
 
 
 def per_device(queries, key_rows, value_rows, grad_out):
-    q_all, k_all, v_all, d_all = (
-        lax.all_to_all(queries, "head", split_axis=1, concat_axis=0, tiled=True),
-        lax.all_to_all(key_rows, "head", split_axis=1, concat_axis=0, tiled=True),
-        lax.all_to_all(value_rows, "head", split_axis=1, concat_axis=0, tiled=True),
-        lax.all_to_all(grad_out, "head", split_axis=1, concat_axis=0, tiled=True),
+    stacked = jnp.stack([queries, key_rows, value_rows, grad_out])
+    q_all, k_all, v_all, d_all = lax.all_to_all(
+        stacked, "head", split_axis=2, concat_axis=1, tiled=True
     )
     rows_here = q_all.shape[0]
     heads_here = q_all.shape[1] // HEAD_DIM
@@ -47,9 +46,7 @@
     g_blocks = jnp.einsum("ntha,nthb->nhab", d_four, q_four, preferred_element_type=jnp.float32)
     kv_local = jnp.sum(kv_blocks, axis=0)
     g_local = jnp.sum(g_blocks, axis=0)
-    zeros_state = jnp.zeros_like(kv_local)
-    kv_before = entering(kv_local, "ctx", add_states, zeros_state, False)
-    g_after = entering(g_local, "ctx", add_states, zeros_state, True)
+    kv_before, g_after = exclusive_scans(kv_local, g_local, "ctx")
     row_ids = lax.broadcasted_iota(jnp.int32, (nblocks, nblocks), 0)
     col_ids = lax.broadcasted_iota(jnp.int32, (nblocks, nblocks), 1)
     strict_lower = (col_ids < row_ids).astype(jnp.float32)
@@ -86,10 +83,9 @@
     grad_q = grad_q.reshape(flat_shape).astype(jnp.bfloat16)
     grad_k = grad_k.reshape(flat_shape).astype(jnp.bfloat16)
     grad_v = grad_v.reshape(flat_shape).astype(jnp.bfloat16)
-    result_q, result_k, result_v = (
-        lax.all_to_all(grad_q, "head", split_axis=0, concat_axis=1, tiled=True),
-        lax.all_to_all(grad_k, "head", split_axis=0, concat_axis=1, tiled=True),
-        lax.all_to_all(grad_v, "head", split_axis=0, concat_axis=1, tiled=True),
+    grads = jnp.stack([grad_q, grad_k, grad_v])
+    result_q, result_k, result_v = lax.all_to_all(
+        grads, "head", split_axis=1, concat_axis=2, tiled=True
     )
     return (result_q, result_k, result_v)
 

time: 364 us -> 193 us (0.53)
  the two profiles are of different devices: /device:TPU:1 before, /device:TPU:6 now
where the time goes in v1:
time: 193 us
  blocking collectives  66 us (34%)
  starting transfers between devices  55.3 us (29%)
  waiting for transfers between devices  32.2 us (17%)
  local copies, waits for them, and re-layouts  27.6 us (14%)
  matrix products  6.56 us (3%)
  other arithmetic  3.85 us (2%)
    ppermute x6, starting transfers between devices, exclusive_scans(): got_fwd = lax.ppermute(fwd_total, axis, to_right)  43.9 us
    all_to_all x1, blocking collectives, per_device(): lax.all_to_all(stacked, 'head', split_axis=2, concat_axis=1, tiled=True)  35.6 us
    all_to_all x1, blocking collectives, per_device(): lax.all_to_all(grads, 'head', split_axis=1, concat_axis=2, tiled=True)  30.3 us
    ppermute x6, waiting for transfers between devices, exclusive_scans(): got_bwd = lax.ppermute(bwd_total, axis, to_left)  24.1 us
    unnamed x13, local copies, waits for them, and re-layouts  14.3 us
    ppermute x6, starting transfers between devices, exclusive_scans(): got_bwd = lax.ppermute(bwd_total, axis, to_left)  11.3 us
    ppermute x6, waiting for transfers between devices, exclusive_scans(): got_fwd = lax.ppermute(fwd_total, axis, to_right)  8.12 us
    all_to_all x1, local copies, waits for them, and re-layouts, per_device(): lax.all_to_all(stacked, 'head', split_axis=2, concat_axis=1, tiled=True)  5.51 us
  transfers between devices with their start and end apart: 12, of which 7 were waited for; matrix products, arithmetic and copies ran while one was open for 3% of the time, Pallas kernels for 0%

profile of v1, /device:TPU:6, one launch (start us, length us, event | category | flops | bytes accessed | tf_op | source)
XLA Modules:
  0.0 192.5 jit_solution(13614894121044651994)
XLA Ops:
  0.6 1.3 pad_maximum_fusion
  2.0 4.7 %copy.93 = bf16[4,32,4096]{1,0,2:T(4,128)(2,1)} copy(bf16[4,32,4096]{2,1,0:T(8,128)(2,1)S(1)} %pad_maximum_fusion) | data formatting | bytes 2097152 | tf_op jit(solution)/shard_map/stack | solution.py:30
  6.6 7.0 %reshape.73 = bf16[8,2,32768]{2,1,0:T(2,128)(2,1)S(1)} reshape(bf16[4096,4,32]{2,1,0:T(4,128)(2,1)} %bitcast.57) | data formatting | bytes 2097152
  13.6 35.6 %all_to_all.30 = bf16[8,2,32768]{2,1,0:T(2,128)(2,1)S(1)} all-to-all(bf16[8,2,32768]{2,1,0:T(2,128)(2,1)S(1)} %reshape.73), channel_id=1, replica_groups=mesh['ctx'=64,'head'=8] {'head'}, dimensions={0} | all-to-all | bytes 2097152 | tf_op jit(solution)/shard_map/all_to_all | solution.py:31
  49.2 4.5 %reshape.74 = bf16[4096,4,32]{2,1,0:T(4,128)(2,1)} reshape(bf16[8,2,32768]{2,1,0:T(2,128)(2,1)S(1)} %all_to_all.30) | data formatting | bytes 2097152
  53.7 5.5 %copy.94 = bf16[4,32,8,512]{3,1,2,0:T(8,128)(2,1)S(1)} copy(bf16[4,32,8,512]{1,0,3,2:T(4,128)(2,1)} %bitcast.58) | data formatting | bytes 2097152 | tf_op jit(solution)/shard_map/all_to_all | solution.py:31
  59.2 0.1 fusion.52
  59.3 0.1 reshape_unstack.12
  59.4 0.1 reshape_unstack.14
  59.5 0.3 fusion.55
  59.8 1.9 collective-permute-start
  61.7 0.1 reshape_unstack.13
  61.8 0.2 copy.105
  62.0 0.1 reshape_unstack.15
  62.0 0.2 fusion.54
  62.3 3.6 %collective-permute-start.6 = (f32[4,128,128]{2,1,0:T(8,128)S(1)}, f32[4,128,128]{2,1,0:T(8,128)S(1)}, u32[]{:S(2)}, u32[]{:S(2)}) collective-permute-start(f32[4,128,128]{2,1,0:T(8,128)S(1)} %get-tuple-element.10), channel_id=1, source_target_pairs={{8,0},{16,8},{24,16},{32,24},{40,32},{48,40},{56,48},{64,56},{72,6... | collective-permute-start | bytes 786440 | tf_op jit(solution)/shard_map/ppermute | solution.py:19
  65.9 1.5 collective-permute-done
  67.5 6.3 %collective-permute-start.1 = (f32[4,128,128]{2,1,0:T(8,128)S(1)}, f32[4,128,128]{2,1,0:T(8,128)S(1)}, u32[]{:S(2)}, u32[]{:S(2)}) collective-permute-start(f32[4,128,128]{2,1,0:T(8,128)S(1)} %add.88), channel_id=1, source_target_pairs={{0,16},{8,24},{16,32},{24,40},{32,48},{40,56},{48,64},{56,72},{64,... | collective-permute-start | bytes 786440 | tf_op jit(solution)/shard_map/ppermute | solution.py:18
  73.8 0.0 collective-permute-done.6
  73.9 1.9 collective-permute-start.7
  75.8 1.9 collective-permute-done.1
  77.7 4.2 %collective-permute-start.2 = (f32[4,128,128]{2,1,0:T(8,128)S(1)}, f32[4,128,128]{2,1,0:T(8,128)S(1)}, u32[]{:S(2)}, u32[]{:S(2)}) collective-permute-start(f32[4,128,128]{2,1,0:T(8,128)S(1)} %add.90), channel_id=1, source_target_pairs={{0,32},{8,40},{16,48},{24,56},{32,64},{40,72},{48,80},{56,88},{64,... | collective-permute-start | bytes 786440 | tf_op jit(solution)/shard_map/ppermute | solution.py:18
  81.9 8.9 %collective-permute-done.7 = f32[4,128,128]{2,1,0:T(8,128)S(1)} collective-permute-done((f32[4,128,128]{2,1,0:T(8,128)S(1)}, f32[4,128,128]{2,1,0:T(8,128)S(1)}, u32[]{:S(2)}, u32[]{:S(2)}) %collective-permute-start.7) | collective-permute-done | bytes 262176 | tf_op jit(solution)/shard_map/ppermute | solution.py:19
  90.9 1.9 collective-permute-start.8
  92.8 0.0 collective-permute-done.2
  92.8 4.3 %collective-permute-start.3 = (f32[4,128,128]{2,1,0:T(8,128)S(1)}, f32[4,128,128]{2,1,0:T(8,128)S(1)}, u32[]{:S(2)}, u32[]{:S(2)}) collective-permute-start(f32[4,128,128]{2,1,0:T(8,128)S(1)} %add.92), channel_id=1, source_target_pairs={{0,64},{8,72},{16,80},{24,88},{32,96},{40,104},{48,112},{56,120},{... | collective-permute-start | bytes 786440 | tf_op jit(solution)/shard_map/ppermute | solution.py:18
  97.2 5.4 %collective-permute-done.8 = f32[4,128,128]{2,1,0:T(8,128)S(1)} collective-permute-done((f32[4,128,128]{2,1,0:T(8,128)S(1)}, f32[4,128,128]{2,1,0:T(8,128)S(1)}, u32[]{:S(2)}, u32[]{:S(2)}) %collective-permute-start.8) | collective-permute-done | bytes 262176 | tf_op jit(solution)/shard_map/ppermute | solution.py:19
  102.6 1.3 collective-permute-start.9
  103.9 7.7 %collective-permute-start.4 = (f32[4,128,128]{2,1,0:T(8,128)S(1)}, f32[4,128,128]{2,1,0:T(8,128)S(1)}, u32[]{:S(2)}, u32[]{:S(2)}) collective-permute-start(f32[4,128,128]{2,1,0:T(8,128)S(1)} %add.94), channel_id=1, source_target_pairs={{0,128},{8,136},{16,144},{24,152},{32,160},{40,168},{48,176},{56,1... | collective-permute-start | bytes 786440 | tf_op jit(solution)/shard_map/ppermute | solution.py:18
  111.7 0.3 fusion.4
  112.0 0.0 copy-start.1
  112.0 1.3 collective-permute-start.10
  113.3 2.3 %collective-permute-done.4 = f32[4,128,128]{2,1,0:T(8,128)S(1)} collective-permute-done((f32[4,128,128]{2,1,0:T(8,128)S(1)}, f32[4,128,128]{2,1,0:T(8,128)S(1)}, u32[]{:S(2)}, u32[]{:S(2)}) %collective-permute-start.4) | collective-permute-done | bytes 262176 | tf_op jit(solution)/shard_map/ppermute | solution.py:18
  115.7 19.5 %collective-permute-start.5 = (f32[4,128,128]{2,1,0:T(8,128)S(1)}, f32[4,128,128]{2,1,0:T(8,128)S(1)}, u32[]{:S(2)}, u32[]{:S(2)}) collective-permute-start(f32[4,128,128]{2,1,0:T(8,128)S(1)} %add.96), channel_id=1, source_target_pairs={{0,256},{8,264},{16,272},{24,280},{32,288},{40,296},{48,304},{56,3... | collective-permute-start | bytes 786440 | tf_op jit(solution)/shard_map/ppermute | solution.py:18
  135.3 0.3 fusion.28
  135.6 0.3 fusion.18
  135.9 0.0 copy-start.2
  135.9 0.7 copy-done.2
  136.6 0.7 add.109
  137.3 1.3 collective-permute-start.11
  138.6 2.4 %collective-permute-done.5 = f32[4,128,128]{2,1,0:T(8,128)S(1)} collective-permute-done((f32[4,128,128]{2,1,0:T(8,128)S(1)}, f32[4,128,128]{2,1,0:T(8,128)S(1)}, u32[]{:S(2)}, u32[]{:S(2)}) %collective-permute-start.5) | collective-permute-done | bytes 262176 | tf_op jit(solution)/shard_map/ppermute | solution.py:18
  141.0 0.1 add_add_fusion.1
  141.1 1.4 broadcast_add_fusion.1
  142.5 0.6 fusion.9
  143.1 0.2 copy.103
  143.3 0.8 convert_element_type.70
  144.1 9.8 %collective-permute-done.11 = f32[4,128,128]{2,1,0:T(8,128)} collective-permute-done((f32[4,128,128]{2,1,0:T(8,128)}, f32[4,128,128]{2,1,0:T(8,128)}, u32[]{:S(2)}, u32[]{:S(2)}) %collective-permute-start.11) | collective-permute-done | bytes 262176 | tf_op jit(solution)/shard_map/ppermute | solution.py:19
  153.9 1.3 add_add_fusion
  155.2 1.4 broadcast_add_fusion
  156.6 0.7 convolution_multiply_fusion.2
  157.2 0.6 fusion.8
  157.8 0.2 copy.110
  158.1 0.1 convert_element_type.73
  158.2 0.5 fusion.7
  158.7 0.2 copy.116
  158.9 0.1 convert_element_type.77
  159.0 0.1 pad_maximum_fusion.1
  159.1 0.7 copy.117
  159.8 30.3 %all_to_all.31 = bf16[3,256,512]{2,0,1:T(4,128)(2,1)S(1)} all-to-all(bf16[3,256,512]{2,0,1:T(4,128)(2,1)S(1)} %copy.117), channel_id=1, replica_groups=mesh['ctx'=64,'head'=8] {'head'}, dimensions={1} | all-to-all | bytes 1572864 | tf_op jit(solution)/shard_map/all_to_all | solution.py:87
  190.1 0.2 copy.118
  190.3 0.1 fusion.53
  190.4 0.7 copy.124
  191.1 0.7 copy.125
  191.8 0.7 copy.126
  (19 shorter events, 0.4 us)
Async XLA Ops:
  59.8 7.7 %collective-permute-start = (f32[4,128,128]{2,1,0:T(8,128)S(1)}, f32[4,128,128]{2,1,0:T(8,128)S(1)}, u32[]{:S(2)}, u32[]{:S(2)}) collective-permute-start(f32[4,128,128]{2,1,0:T(8,128)S(1)} %get-tuple-element.12), channel_id=1, source_target_pairs={{0,8},{8,16},{16,24},{24,32},{32,40},{40,48},{48,56},{56,64},{64,7... | collective-permute-start | bytes 786440 | tf_op jit(solution)/shard_map/ppermute | solution.py:18
  62.3 11.5 %collective-permute-start.6 = (f32[4,128,128]{2,1,0:T(8,128)S(1)}, f32[4,128,128]{2,1,0:T(8,128)S(1)}, u32[]{:S(2)}, u32[]{:S(2)}) collective-permute-start(f32[4,128,128]{2,1,0:T(8,128)S(1)} %get-tuple-element.10), channel_id=1, source_target_pairs={{8,0},{16,8},{24,16},{32,24},{40,32},{48,40},{56,48},{64,56},{72,6... | collective-permute-start | bytes 786440 | tf_op jit(solution)/shard_map/ppermute | solution.py:19
  67.5 10.2 %collective-permute-start.1 = (f32[4,128,128]{2,1,0:T(8,128)S(1)}, f32[4,128,128]{2,1,0:T(8,128)S(1)}, u32[]{:S(2)}, u32[]{:S(2)}) collective-permute-start(f32[4,128,128]{2,1,0:T(8,128)S(1)} %add.88), channel_id=1, source_target_pairs={{0,16},{8,24},{16,32},{24,40},{32,48},{40,56},{48,64},{56,72},{64,... | collective-permute-start | bytes 786440 | tf_op jit(solution)/shard_map/ppermute | solution.py:18
  73.9 17.0 %collective-permute-start.7 = (f32[4,128,128]{2,1,0:T(8,128)S(1)}, f32[4,128,128]{2,1,0:T(8,128)S(1)}, u32[]{:S(2)}, u32[]{:S(2)}) collective-permute-start(f32[4,128,128]{2,1,0:T(8,128)S(1)} %add.101), channel_id=1, source_target_pairs={{16,0},{24,8},{32,16},{40,24},{48,32},{56,40},{64,48},{72,56},{80,... | collective-permute-start | bytes 786440 | tf_op jit(solution)/shard_map/ppermute | solution.py:19
  77.7 15.1 %collective-permute-start.2 = (f32[4,128,128]{2,1,0:T(8,128)S(1)}, f32[4,128,128]{2,1,0:T(8,128)S(1)}, u32[]{:S(2)}, u32[]{:S(2)}) collective-permute-start(f32[4,128,128]{2,1,0:T(8,128)S(1)} %add.90), channel_id=1, source_target_pairs={{0,32},{8,40},{16,48},{24,56},{32,64},{40,72},{48,80},{56,88},{64,... | collective-permute-start | bytes 786440 | tf_op jit(solution)/shard_map/ppermute | solution.py:18
  90.9 11.7 %collective-permute-start.8 = (f32[4,128,128]{2,1,0:T(8,128)S(1)}, f32[4,128,128]{2,1,0:T(8,128)S(1)}, u32[]{:S(2)}, u32[]{:S(2)}) collective-permute-start(f32[4,128,128]{2,1,0:T(8,128)S(1)} %add.103), channel_id=1, source_target_pairs={{32,0},{40,8},{48,16},{56,24},{64,32},{72,40},{80,48},{88,56},{96,... | collective-permute-start | bytes 786440 | tf_op jit(solution)/shard_map/ppermute | solution.py:19
  92.8 11.0 %collective-permute-start.3 = (f32[4,128,128]{2,1,0:T(8,128)S(1)}, f32[4,128,128]{2,1,0:T(8,128)S(1)}, u32[]{:S(2)}, u32[]{:S(2)}) collective-permute-start(f32[4,128,128]{2,1,0:T(8,128)S(1)} %add.92), channel_id=1, source_target_pairs={{0,64},{8,72},{16,80},{24,88},{32,96},{40,104},{48,112},{56,120},{... | collective-permute-start | bytes 786440 | tf_op jit(solution)/shard_map/ppermute | solution.py:18
  102.5 9.1 %copy-start = (f32[4,128,128]{2,1,0:T(8,128)}, f32[4,128,128]{2,1,0:T(8,128)S(1)}, u32[]{:S(2)}) copy-start(f32[4,128,128]{2,1,0:T(8,128)S(1)} %collective-permute-done.8) | copy-start | bytes 786436
  102.6 9.4 %collective-permute-start.9 = (f32[4,128,128]{2,1,0:T(8,128)S(1)}, f32[4,128,128]{2,1,0:T(8,128)S(1)}, u32[]{:S(2)}, u32[]{:S(2)}) collective-permute-start(f32[4,128,128]{2,1,0:T(8,128)S(1)} %add.105), channel_id=1, source_target_pairs={{64,0},{72,8},{80,16},{88,24},{96,32},{104,40},{112,48},{120,56},{... | collective-permute-start | bytes 786440 | tf_op jit(solution)/shard_map/ppermute | solution.py:19
  103.9 11.8 %collective-permute-start.4 = (f32[4,128,128]{2,1,0:T(8,128)S(1)}, f32[4,128,128]{2,1,0:T(8,128)S(1)}, u32[]{:S(2)}, u32[]{:S(2)}) collective-permute-start(f32[4,128,128]{2,1,0:T(8,128)S(1)} %add.94), channel_id=1, source_target_pairs={{0,128},{8,136},{16,144},{24,152},{32,160},{40,168},{48,176},{56,1... | collective-permute-start | bytes 786440 | tf_op jit(solution)/shard_map/ppermute | solution.py:18
  112.0 23.9 %copy-start.1 = (f32[4,128,128]{2,1,0:T(8,128)}, f32[4,128,128]{2,1,0:T(8,128)S(1)}, u32[]{:S(2)}) copy-start(f32[4,128,128]{2,1,0:T(8,128)S(1)} %collective-permute-done.9) | copy-start | bytes 786436
  112.0 23.8 %collective-permute-start.10 = (f32[4,128,128]{2,1,0:T(8,128)S(1)}, f32[4,128,128]{2,1,0:T(8,128)S(1)}, u32[]{:S(2)}, u32[]{:S(2)}) collective-permute-start(f32[4,128,128]{2,1,0:T(8,128)S(1)} %add.107), channel_id=1, source_target_pairs={{128,0},{136,8},{144,16},{152,24},{160,32},{168,40},{176,48},{184,... | collective-permute-start | bytes 786440 | tf_op jit(solution)/shard_map/ppermute | solution.py:19
  115.7 25.3 %collective-permute-start.5 = (f32[4,128,128]{2,1,0:T(8,128)S(1)}, f32[4,128,128]{2,1,0:T(8,128)S(1)}, u32[]{:S(2)}, u32[]{:S(2)}) collective-permute-start(f32[4,128,128]{2,1,0:T(8,128)S(1)} %add.96), channel_id=1, source_target_pairs={{0,256},{8,264},{16,272},{24,280},{32,288},{40,296},{48,304},{56,3... | collective-permute-start | bytes 786440 | tf_op jit(solution)/shard_map/ppermute | solution.py:18
  135.9 0.7 copy-start.2
  137.3 16.6 %collective-permute-start.11 = (f32[4,128,128]{2,1,0:T(8,128)}, f32[4,128,128]{2,1,0:T(8,128)}, u32[]{:S(2)}, u32[]{:S(2)}) collective-permute-start(f32[4,128,128]{2,1,0:T(8,128)} %add.109), channel_id=1, source_target_pairs={{256,0},{264,8},{272,16},{280,24},{288,32},{296,40},{304,48},{312,... | collective-permute-start | bytes 786440 | tf_op jit(solution)/shard_map/ppermute | solution.py:19
  155.2 3.8 %copy-start.3 = (bf16[1,256,512]{2,1,0:T(8,128)(2,1)S(1)}, bf16[1,256,512]{2,1,0:T(8,128)(2,1)}, u32[]{:S(2)}) copy-start(bf16[1,256,512]{2,1,0:T(8,128)(2,1)} %convert_element_type.70) | copy-start | bytes 786436

commit v2 on v1

--- a/solution.py
+++ b/solution.py
@@ -1,29 +1,134 @@
+import functools
+
 import jax
 import jax.numpy as jnp
 from jax import lax
+from jax.experimental import pallas as pl
+from jax.experimental.pallas import tpu as pltpu
 from jax.sharding import PartitionSpec as P
 
 HEAD_DIM = 128
 GROUP = 128
 
 
+MESH = pl.DeviceIdType.MESH
+
+
+def scan_kernel(count, rounds, fwd_in, bwd_in, fwd_out, bwd_out,
+                fwd_tot, bwd_tot, fwd_got, bwd_got, send_sems, recv_sems):
+    me = lax.axis_index("ctx")
+    head = lax.axis_index("head")
+    barrier = pltpu.get_barrier_semaphore()
+    for k in range(rounds):
+        shift = 1 << k
+
+        @pl.when(me + shift < count)
+        def _():
+            pl.semaphore_signal(barrier, inc=1, device_id=(me + shift, head), device_id_type=MESH)
+
+        @pl.when(me >= shift)
+        def _():
+            pl.semaphore_signal(barrier, inc=1, device_id=(me - shift, head), device_id_type=MESH)
+
+    peers = 0
+    for k in range(rounds):
+        shift = 1 << k
+        peers = peers + (me + shift < count).astype(jnp.int32) + (me >= shift).astype(jnp.int32)
+    pl.semaphore_wait(barrier, peers)
+
+    fwd_out[...] = jnp.zeros_like(fwd_out)
+    bwd_out[...] = jnp.zeros_like(bwd_out)
+
+    def copies(k):
+        shift = 1 << k
+        src_f = fwd_in if k == 0 else fwd_tot.at[k - 1]
+        src_b = bwd_in if k == 0 else bwd_tot.at[k - 1]
+        to_right = pltpu.make_async_remote_copy(
+            src_ref=src_f, dst_ref=fwd_got.at[k], send_sem=send_sems.at[0, k],
+            recv_sem=recv_sems.at[0, k], device_id=(me + shift, head), device_id_type=MESH)
+        to_left = pltpu.make_async_remote_copy(
+            src_ref=src_b, dst_ref=bwd_got.at[k], send_sem=send_sems.at[1, k],
+            recv_sem=recv_sems.at[1, k], device_id=(me - shift, head), device_id_type=MESH)
+        return src_f, src_b, to_right, to_left
+
+    for k in range(rounds):
+        shift = 1 << k
+        src_f, src_b, to_right, to_left = copies(k)
+
+        @pl.when(me + shift < count)
+        def _():
+            to_right.start()
+
+        @pl.when(me >= shift)
+        def _():
+            to_left.start()
+
+        last = k == rounds - 1
+
+        @pl.when(me >= shift)
+        def _():
+            to_right.wait_recv()
+            got = fwd_got[k]
+            fwd_out[...] += got
+            if not last:
+                fwd_tot[k] = src_f[...] + got
+
+        @pl.when(me < shift)
+        def _():
+            if not last:
+                fwd_tot[k] = src_f[...]
+
+        @pl.when(me + shift < count)
+        def _():
+            to_left.wait_recv()
+            got = bwd_got[k]
+            bwd_out[...] += got
+            if not last:
+                bwd_tot[k] = src_b[...] + got
+
+        @pl.when(me + shift >= count)
+        def _():
+            if not last:
+                bwd_tot[k] = src_b[...]
+
+    for k in range(rounds):
+        shift = 1 << k
+        src_f, src_b, to_right, to_left = copies(k)
+
+        @pl.when(me + shift < count)
+        def _():
+            to_right.wait_send()
+
+        @pl.when(me >= shift)
+        def _():
+            to_left.wait_send()
+
+
 def exclusive_scans(forward_part, backward_part, axis):
     count = lax.axis_size(axis)
-    fwd_total, fwd_excl = forward_part, jnp.zeros_like(forward_part)
-    bwd_total, bwd_excl = backward_part, jnp.zeros_like(backward_part)
-    shift = 1
-    while shift < count:
-        to_right = [(i, i + shift) for i in range(count - shift)]
-        to_left = [(i + shift, i) for i in range(count - shift)]
-        got_fwd = lax.ppermute(fwd_total, axis, to_right)
-        got_bwd = lax.ppermute(bwd_total, axis, to_left)
-        fwd_excl = fwd_excl + got_fwd
-        bwd_excl = bwd_excl + got_bwd
-        if shift * 2 < count:
-            fwd_total = fwd_total + got_fwd
-            bwd_total = bwd_total + got_bwd
-        shift *= 2
-    return fwd_excl, bwd_excl
+    rounds = max(1, (count - 1).bit_length())
+    shape = forward_part.shape
+    fwd = forward_part.reshape(-1, shape[-1])
+    bwd = backward_part.reshape(-1, shape[-1])
+    rows, cols = fwd.shape
+    vmem = pl.BlockSpec(memory_space=pltpu.VMEM)
+    fwd_excl, bwd_excl = pl.pallas_call(
+        functools.partial(scan_kernel, count, rounds),
+        out_shape=(jax.ShapeDtypeStruct(fwd.shape, fwd.dtype),) * 2,
+        in_specs=[vmem, vmem],
+        out_specs=(vmem, vmem),
+        scratch_shapes=[
+            pltpu.VMEM((rounds, rows, cols), jnp.float32),
+            pltpu.VMEM((rounds, rows, cols), jnp.float32),
+            pltpu.VMEM((rounds, rows, cols), jnp.float32),
+            pltpu.VMEM((rounds, rows, cols), jnp.float32),
+            pltpu.SemaphoreType.DMA((2, rounds)),
+            pltpu.SemaphoreType.DMA((2, rounds)),
+        ],
+        compiler_params=pltpu.CompilerParams(collective_id=0, has_side_effects=True,
+                                             vmem_limit_bytes=48 * 1024 * 1024),
+    )(fwd, bwd)
+    return fwd_excl.reshape(shape), bwd_excl.reshape(shape)
 
 
 def per_device(queries, key_rows, value_rows, grad_out):

time: 193 us -> 179 us (0.927)
  Pallas kernels: 0 us -> 76.5 us
  starting transfers between devices: 55.3 us -> 7.1 us
  blocking collectives: 66 us -> 30.9 us
  waiting for transfers between devices: 32.2 us -> 28.7 us
  other arithmetic: 3.85 us -> 1.43 us
    pallas_call x0 -> x1, Pallas kernels: none -> 76.5 us  [exclusive_scans(): pl.pallas_call(functools.partial(scan_kernel, count, rounds), out_shape=(...]
    ppermute x12 -> x0, starting transfers between devices: 55.3 us -> none  [the longest x6 43.9 us: exclusive_scans(): got_fwd = lax.ppermute(fwd_total, axis, to_right)]
    all_to_all x1 -> x0, blocking collectives: 35.6 us -> none  [per_device(): lax.all_to_all(stacked, 'head', split_axis=2, concat_axis=1, tiled=True)]
    ppermute x12 -> x0, waiting for transfers between devices: 32.2 us -> none  [the longest x6 24.1 us: exclusive_scans(): got_bwd = lax.ppermute(bwd_total, axis, to_left)]
    all_to_all x0 -> x1, waiting for transfers between devices: none -> 28.7 us  [per_device(): lax.all_to_all(stacked, 'head', split_axis=2, concat_axis=1, tiled=True)]
    all_to_all x0 -> x1, starting transfers between devices: none -> 7.1 us  [per_device(): lax.all_to_all(stacked, 'head', split_axis=2, concat_axis=1, tiled=True)]
    add x12 -> x0, other arithmetic: 2.42 us -> none  [the longest x1 1.26 us: exclusive_scans(): bwd_excl = bwd_excl + got_bwd]
    unnamed x13 -> x5, local copies, waits for them, and re-layouts: 14.3 us -> 14.5 us
  transfers between devices with their start and end apart: 12 -> 1, of which waited for: 7 -> 1; matrix products, arithmetic and copies ran while one was open for 3% -> 0% of each run, Pallas kernels for 0% -> 0%
where the time goes in v2:
time: 179 us
  Pallas kernels  76.5 us (43%)
  blocking collectives  30.9 us (17%)
  waiting for transfers between devices  28.7 us (16%)
  local copies, waits for them, and re-layouts  27 us (15%)
  starting transfers between devices  7.1 us (4%)
  matrix products  6.47 us (4%)
    pallas_call x1, Pallas kernels, exclusive_scans(): pl.pallas_call(functools.partial(scan_kernel, count, rounds), out_shape=(...  76.5 us
    all_to_all x1, blocking collectives, per_device(): lax.all_to_all(grads, 'head', split_axis=1, concat_axis=2, tiled=True)  30.9 us
    all_to_all x1, waiting for transfers between devices, per_device(): lax.all_to_all(stacked, 'head', split_axis=2, concat_axis=1, tiled=True)  28.7 us
    unnamed x5, local copies, waits for them, and re-layouts  14.5 us
    all_to_all x1, starting transfers between devices, per_device(): lax.all_to_all(stacked, 'head', split_axis=2, concat_axis=1, tiled=True)  7.1 us
    all_to_all x1, local copies, waits for them, and re-layouts, per_device(): lax.all_to_all(stacked, 'head', split_axis=2, concat_axis=1, tiled=True)  5.51 us
    another operation x1, local copies, waits for them, and re-layouts, per_device(): stacked = jnp.stack([queries, key_rows, value_rows, grad_out])  4.69 us
  transfers between devices with their start and end apart: 1, of which 1 were waited for; matrix products, arithmetic and copies ran while one was open for 0% of the time, Pallas kernels for 0%

profile of v2, /device:TPU:6, one launch (start us, length us, event | category | flops | bytes accessed | tf_op | source)
XLA Modules:
  0.0 178.9 jit_solution(689943659559046470)
XLA Ops:
  0.6 1.3 pad_maximum_fusion
  2.0 4.7 %copy.95 = bf16[4,32,4096]{1,0,2:T(4,128)(2,1)} copy(bf16[4,32,4096]{2,1,0:T(8,128)(2,1)S(1)} %pad_maximum_fusion) | data formatting | bytes 2097152 | tf_op jit(solution)/shard_map/stack | solution.py:135
  6.6 7.8 %reshape.81 = bf16[8,2,32768]{2,1,0:T(2,128)(2,1)} reshape(bf16[4096,4,32]{2,1,0:T(4,128)(2,1)} %bitcast.59) | data formatting | bytes 2097152
  14.4 7.1 %all-to-all-start = ((bf16[8,2,32768]{2,1,0:T(2,128)(2,1)}), bf16[8,2,32768]{2,1,0:T(2,128)(2,1)S(1)}, u32[]{:S(2)}, u32[]{:S(2)}) async-start(bf16[8,2,32768]{2,1,0:T(2,128)(2,1)} %reshape.81), calls=%async_computation | async-start | bytes 2097152 | tf_op jit(solution)/shard_map/all_to_all | solution.py:136
  21.6 28.7 %all-to-all-done = bf16[8,2,32768]{2,1,0:T(2,128)(2,1)S(1)} async-done(((bf16[8,2,32768]{2,1,0:T(2,128)(2,1)}), bf16[8,2,32768]{2,1,0:T(2,128)(2,1)S(1)}, u32[]{:S(2)}, u32[]{:S(2)}) %all-to-all-start) | async-done | bytes 1048608 | tf_op jit(solution)/shard_map/all_to_all | solution.py:136
  50.3 4.5 %reshape.82 = bf16[4096,4,32]{2,1,0:T(4,128)(2,1)} reshape(bf16[8,2,32768]{2,1,0:T(2,128)(2,1)S(1)} %all-to-all-done) | data formatting | bytes 2097152
  54.8 5.5 %copy.96 = bf16[4,32,8,512]{3,1,2,0:T(8,128)(2,1)S(1)} copy(bf16[4,32,8,512]{1,0,3,2:T(4,128)(2,1)} %bitcast.60) | data formatting | bytes 2097152 | tf_op jit(solution)/shard_map/all_to_all | solution.py:136
  60.3 0.1 fusion.44
  60.4 0.1 reshape_unstack.12
  60.5 0.1 reshape_unstack.14
  60.5 0.1 reshape_unstack.13
  60.6 0.2 copy.102
  60.8 0.1 reshape_unstack.15
  60.9 0.3 fusion.46
  61.1 0.2 fusion.47
  61.4 76.5 %shard_map.67 = (f32[512,128]{1,0:T(8,128)S(1)}, f32[512,128]{1,0:T(8,128)S(1)}) custom-call(f32[512,128]{1,0:T(8,128)S(1)} %bitcast.55, f32[512,128]{1,0:T(8,128)S(1)} %bitcast.56), custom_call_target="tpu_custom_call" | custom-call | tf_op jit(solution)/shard_map/pallas_call | solution.py:115
  137.8 1.4 convolution_add_fusion
  139.2 0.7 convolution_multiply_fusion.2
  139.9 0.6 fusion.14
  140.5 0.5 fusion.7
  141.0 0.2 copy.118
  141.2 0.1 convert_element_type.77
  141.3 1.4 convolution_add_fusion.1
  142.6 0.6 fusion.10
  143.2 0.3 fusion.4
  143.5 0.3 fusion.9
  143.9 0.2 copy.107
  144.1 0.1 convert_element_type.70
  144.2 0.3 fusion.8
  144.5 0.2 copy.112
  144.7 0.1 convert_element_type.73
  144.8 0.1 pad_maximum_fusion.1
  144.9 0.7 copy.119
  145.6 30.9 %all_to_all.30 = bf16[3,256,512]{2,0,1:T(4,128)(2,1)S(1)} all-to-all(bf16[3,256,512]{2,0,1:T(4,128)(2,1)S(1)} %copy.119), channel_id=1, replica_groups=mesh['ctx'=64,'head'=8] {'head'}, dimensions={1} | all-to-all | bytes 1572864 | tf_op jit(solution)/shard_map/all_to_all | solution.py:192
  176.4 0.2 copy.120
  176.6 0.1 fusion.45
  176.7 0.7 copy.126
  177.4 0.7 copy.127
  178.1 0.7 copy.128
  (2 shorter events, 0.0 us)
Async XLA Ops:
  14.4 35.8 %all-to-all-start = ((bf16[8,2,32768]{2,1,0:T(2,128)(2,1)}), bf16[8,2,32768]{2,1,0:T(2,128)(2,1)S(1)}, u32[]{:S(2)}, u32[]{:S(2)}) async-start(bf16[8,2,32768]{2,1,0:T(2,128)(2,1)} %reshape.81), calls=%async_computation | async-start | bytes 2097152 | tf_op jit(solution)/shard_map/all_to_all | solution.py:136

commit v3 on v2

--- a/solution.py
+++ b/solution.py
@@ -102,6 +102,67 @@
         @pl.when(me >= shift)
         def _():
             to_left.wait_send()
+
+
+def exchange_kernel(count, n_arrays, src_cut, dst_cut, *refs):
+    srcs = refs[:n_arrays]
+    dsts = refs[n_arrays:2 * n_arrays]
+    send_sems, recv_sems, local_sems = refs[2 * n_arrays:]
+    me = lax.axis_index("head")
+    place = lax.axis_index("ctx")
+    barrier = pltpu.get_barrier_semaphore()
+    for j in range(count):
+        @pl.when(me != j)
+        def _():
+            pl.semaphore_signal(barrier, inc=1, device_id=(place, j), device_id_type=MESH)
+    pl.semaphore_wait(barrier, count - 1)
+
+    def remote(a, j, dst_index):
+        return pltpu.make_async_remote_copy(
+            src_ref=src_cut(srcs[a], j), dst_ref=dst_cut(dsts[a], dst_index),
+            send_sem=send_sems.at[a, j], recv_sem=recv_sems.at[a, me],
+            device_id=(place, j), device_id_type=MESH)
+
+    for a in range(n_arrays):
+        local = pltpu.make_async_copy(src_cut(srcs[a], me), dst_cut(dsts[a], me), local_sems.at[a])
+        local.start()
+    for step in range(1, count):
+        for a in range(n_arrays):
+            j_dyn = lax.rem(me + step, count)
+            for j in range(count):
+                @pl.when(j_dyn == j)
+                def _():
+                    remote(a, j, me).start()
+    for a in range(n_arrays):
+        pltpu.make_async_copy(src_cut(srcs[a], me), dst_cut(dsts[a], me), local_sems.at[a]).wait()
+    for a in range(n_arrays):
+        for j in range(count):
+            @pl.when(me != j)
+            def _():
+                copy = pltpu.make_async_remote_copy(
+                    src_ref=src_cut(srcs[a], j), dst_ref=dst_cut(dsts[a], j),
+                    send_sem=send_sems.at[a, j], recv_sem=recv_sems.at[a, j],
+                    device_id=(place, j), device_id_type=MESH)
+                copy.wait_send()
+                copy.wait_recv()
+
+
+def exchange(arrays, out_shape, src_cut, dst_cut, collective_id):
+    count = lax.axis_size("head")
+    n_arrays = len(arrays)
+    anywhere = pl.BlockSpec(memory_space=pl.ANY)
+    return pl.pallas_call(
+        functools.partial(exchange_kernel, count, n_arrays, src_cut, dst_cut),
+        out_shape=tuple(jax.ShapeDtypeStruct(out_shape, arrays[0].dtype) for _ in arrays),
+        in_specs=[anywhere] * n_arrays,
+        out_specs=tuple(anywhere for _ in arrays),
+        scratch_shapes=[
+            pltpu.SemaphoreType.DMA((n_arrays, count)),
+            pltpu.SemaphoreType.DMA((n_arrays, count)),
+            pltpu.SemaphoreType.DMA((n_arrays,)),
+        ],
+        compiler_params=pltpu.CompilerParams(collective_id=collective_id, has_side_effects=True),
+    )(*arrays)
 
 
 def exclusive_scans(forward_part, backward_part, axis):
@@ -132,9 +193,15 @@
 
 
 def per_device(queries, key_rows, value_rows, grad_out):
-    stacked = jnp.stack([queries, key_rows, value_rows, grad_out])
-    q_all, k_all, v_all, d_all = lax.all_to_all(
-        stacked, "head", split_axis=2, concat_axis=1, tiled=True
+    count = lax.axis_size("head")
+    rows_in, width = queries.shape
+    cols = width // count
+    q_all, k_all, v_all, d_all = exchange(
+        (queries, key_rows, value_rows, grad_out),
+        (rows_in * count, cols),
+        lambda ref, j: ref.at[:, pl.ds(j * cols, cols)],
+        lambda ref, j: ref.at[pl.ds(j * rows_in, rows_in), :],
+        1,
     )
     rows_here = q_all.shape[0]
     heads_here = q_all.shape[1] // HEAD_DIM
@@ -188,9 +255,12 @@
     grad_q = grad_q.reshape(flat_shape).astype(jnp.bfloat16)
     grad_k = grad_k.reshape(flat_shape).astype(jnp.bfloat16)
     grad_v = grad_v.reshape(flat_shape).astype(jnp.bfloat16)
-    grads = jnp.stack([grad_q, grad_k, grad_v])
-    result_q, result_k, result_v = lax.all_to_all(
-        grads, "head", split_axis=1, concat_axis=2, tiled=True
+    result_q, result_k, result_v = exchange(
+        (grad_q, grad_k, grad_v),
+        (rows_in, width),
+        lambda ref, j: ref.at[pl.ds(j * rows_in, rows_in), :],
+        lambda ref, j: ref.at[:, pl.ds(j * cols, cols)],
+        2,
     )
     return (result_q, result_k, result_v)
 

time: 179 us -> 148 us (0.83)
  the two profiles are of different devices: /device:TPU:6 before, /device:TPU:116 now
where the time goes in v3:
time: 148 us; the launch traced here: 147 us
  Pallas kernels  130 us (88%)
  local copies, waits for them, and re-layouts  9.18 us (6%)
  matrix products  7.13 us (5%)
    pallas_call x1, Pallas kernels, exclusive_scans(): pl.pallas_call(functools.partial(scan_kernel, count, rounds), out_shape=(...  75 us
    pallas_call x2, Pallas kernels, exchange(): pl.pallas_call(functools.partial(exchange_kernel, count, n_arrays, src_cu...  55.3 us
    unnamed x16, local copies, waits for them, and re-layouts  5.77 us

profile of v3, /device:TPU:116, one launch (start us, length us, event | category | flops | bytes accessed | tf_op | source)
XLA Modules:
  0.0 147.4 jit_solution(16483681263444884814)
XLA Ops:
  0.6 30.5 %shard_map.67 = (bf16[256,512]{1,0:T(8,128)(2,1)}, bf16[256,512]{1,0:T(8,128)(2,1)}, bf16[256,512]{1,0:T(8,128)(2,1)}, bf16[256,512]{1,0:T(8,128)(2,1)}) custom-call(bf16[32,4096]{1,0:T(8,128)(2,1)} %refs_0_.1, bf16[32,4096]{1,0:T(8,128)(2,1)} %refs_1_.1, bf16[32,4096]{1,0:T(8,128)(2,1)} %refs_2_.1, bf16[32,4096]{1,0:T(8,128)(2,1)} %refs_3_.1), custom_call_target="tpu_custom_call" | custom-call | tf_op jit(solution)/shard_map/pallas_call | solution.py:154
  31.1 0.0 copy-start.5
  31.1 1.1 reshape.45
  32.2 0.0 copy-done.5
  32.2 0.1 reshape.47
  32.3 0.3 fusion.43
  32.5 1.3 fusion.12
  33.8 0.0 copy-start.2
  33.9 0.2 copy.28
  34.1 0.7 copy-done.2
  34.8 0.1 reshape.46
  34.9 0.0 copy-start.1
  34.9 0.2 copy.12
  35.1 0.7 copy-done.1
  35.8 0.1 reshape.49
  35.9 1.0 fusion.44
  36.9 75.0 %shard_map.68 = (f32[512,128]{1,0:T(8,128)S(1)}, f32[512,128]{1,0:T(8,128)S(1)}) custom-call(f32[512,128]{1,0:T(8,128)S(1)} %bitcast.39, f32[512,128]{1,0:T(8,128)S(1)} %bitcast.40), custom_call_target="tpu_custom_call" | custom-call | tf_op jit(solution)/shard_map/pallas_call | solution.py:176
  111.9 0.1 copy.14
  112.0 0.7 fusion.10
  112.7 0.2 copy.9
  112.9 0.3 fusion.4
  113.2 0.3 fusion.9
  113.5 0.0 copy-start
  113.5 0.2 copy.16
  113.8 0.7 copy.71
  114.5 0.1 copy-done
  114.6 1.3 convolution_add_fusion
  115.9 0.7 convolution_multiply_fusion.2
  116.6 0.4 fusion.7
  117.0 0.2 copy.25
  117.2 0.6 fusion.15
  117.8 0.3 fusion.8
  118.1 0.2 copy.21
  118.3 0.9 copy_bitcast_fusion
  119.1 24.8 %shard_map.69 = (bf16[32,4096]{1,0:T(8,128)(2,1)}, bf16[32,4096]{1,0:T(8,128)(2,1)}, bf16[32,4096]{1,0:T(8,128)(2,1)}) custom-call(bf16[256,512]{1,0:T(8,128)(2,1)} %bitcast.43, bf16[256,512]{1,0:T(8,128)(2,1)} %get-tuple-element.20.refs_1_, bf16[256,512]{1,0:T(8,128)(2,1)} %get-tuple-element.19.refs_2_), custom_call_target="tpu_custom_call" | custom-call | tf_op jit(solution)/shard_map/pallas_call | solution.py:154
  144.0 0.0 copy-start.4
  144.0 1.7 %copy.75 = bf16[32,4096]{1,0:T(8,128)(2,1)} copy(bf16[32,4096]{1,0:T(8,128)(2,1)} %get-tuple-element.24) | data formatting | bytes 524288
  145.7 0.0 copy-done.4
  145.7 0.0 copy-start.3
  145.7 0.7 copy.76
  146.4 0.3 copy-done.3
  146.7 0.7 copy.77
  (2 shorter events, 0.0 us)
Async XLA Ops:
  31.1 1.1 copy-start.5
  33.8 1.0 copy-start.2
  34.9 1.0 copy-start.1
  113.5 1.0 copy-start
  144.0 1.7 %copy-start.4 = (bf16[32,4096]{1,0:T(8,128)(2,1)S(1)}, bf16[32,4096]{1,0:T(8,128)(2,1)}, u32[]{:S(2)}) copy-start(bf16[32,4096]{1,0:T(8,128)(2,1)} %get-tuple-element.25) | copy-start | bytes 786436
  145.7 1.0 copy-start.3

commit v4 on v3

--- a/solution.py
+++ b/solution.py
@@ -14,94 +14,178 @@
 MESH = pl.DeviceIdType.MESH
 
 
-def scan_kernel(count, rounds, fwd_in, bwd_in, fwd_out, bwd_out,
-                fwd_tot, bwd_tot, fwd_got, bwd_got, send_sems, recv_sems):
+def scan_kernel(chips, rounds, half, fwd_in, bwd_in, fwd_out, bwd_out,
+                peer_f, peer_b, tot_f, tot_b, got_f, got_b, ex_f, ex_b, fin_f, fin_b,
+                send_sems, recv_sems):
     me = lax.axis_index("ctx")
     head = lax.axis_index("head")
+    core = lax.rem(me, 2)
+    chip = me // 2
+    partner = me + 1 - 2 * core
     barrier = pltpu.get_barrier_semaphore()
+    pl.semaphore_signal(barrier, inc=1, device_id=(partner, head), device_id_type=MESH)
+    peers = 1
     for k in range(rounds):
         shift = 1 << k
 
-        @pl.when(me + shift < count)
-        def _():
-            pl.semaphore_signal(barrier, inc=1, device_id=(me + shift, head), device_id_type=MESH)
-
-        @pl.when(me >= shift)
-        def _():
-            pl.semaphore_signal(barrier, inc=1, device_id=(me - shift, head), device_id_type=MESH)
-
-    peers = 0
+        @pl.when(chip + shift < chips)
+        def _():
+            pl.semaphore_signal(barrier, inc=1, device_id=(me + 2 * shift, head), device_id_type=MESH)
+
+        @pl.when(chip >= shift)
+        def _():
+            pl.semaphore_signal(barrier, inc=1, device_id=(me - 2 * shift, head), device_id_type=MESH)
+
+        peers = peers + (chip + shift < chips).astype(jnp.int32) + (chip >= shift).astype(jnp.int32)
+    pl.semaphore_wait(barrier, peers)
+
+    def on_chip(src_f, dst_f, src_b, dst_b, slot):
+        return (
+            pltpu.make_async_remote_copy(
+                src_ref=src_f, dst_ref=dst_f, send_sem=send_sems.at[0, slot],
+                recv_sem=recv_sems.at[0, slot], device_id=(partner, head), device_id_type=MESH),
+            pltpu.make_async_remote_copy(
+                src_ref=src_b, dst_ref=dst_b, send_sem=send_sems.at[1, slot],
+                recv_sem=recv_sems.at[1, slot], device_id=(partner, head), device_id_type=MESH),
+        )
+
+    first = on_chip(fwd_in, peer_f, bwd_in, peer_b, 0)
+    for copy in first:
+        copy.start()
+    for copy in first:
+        copy.wait_recv()
+
+    for mine in range(2):
+        rows = pl.ds(mine * half, half)
+
+        @pl.when(core == mine)
+        def _():
+            tot_f[0] = fwd_in[rows, :] + peer_f[rows, :]
+            tot_b[0] = bwd_in[rows, :] + peer_b[rows, :]
+
+    ex_f[...] = jnp.zeros_like(ex_f)
+    ex_b[...] = jnp.zeros_like(ex_b)
+
+    def copies(k):
+        shift = 1 << k
+        to_right = pltpu.make_async_remote_copy(
+            src_ref=tot_f.at[k], dst_ref=got_f.at[k], send_sem=send_sems.at[0, k + 1],
+            recv_sem=recv_sems.at[0, k + 1], device_id=(me + 2 * shift, head), device_id_type=MESH)
+        to_left = pltpu.make_async_remote_copy(
+            src_ref=tot_b.at[k], dst_ref=got_b.at[k], send_sem=send_sems.at[1, k + 1],
+            recv_sem=recv_sems.at[1, k + 1], device_id=(me - 2 * shift, head), device_id_type=MESH)
+        return to_right, to_left
+
     for k in range(rounds):
         shift = 1 << k
-        peers = peers + (me + shift < count).astype(jnp.int32) + (me >= shift).astype(jnp.int32)
-    pl.semaphore_wait(barrier, peers)
-
-    fwd_out[...] = jnp.zeros_like(fwd_out)
-    bwd_out[...] = jnp.zeros_like(bwd_out)
-
-    def copies(k):
-        shift = 1 << k
-        src_f = fwd_in if k == 0 else fwd_tot.at[k - 1]
-        src_b = bwd_in if k == 0 else bwd_tot.at[k - 1]
-        to_right = pltpu.make_async_remote_copy(
-            src_ref=src_f, dst_ref=fwd_got.at[k], send_sem=send_sems.at[0, k],
-            recv_sem=recv_sems.at[0, k], device_id=(me + shift, head), device_id_type=MESH)
-        to_left = pltpu.make_async_remote_copy(
-            src_ref=src_b, dst_ref=bwd_got.at[k], send_sem=send_sems.at[1, k],
-            recv_sem=recv_sems.at[1, k], device_id=(me - shift, head), device_id_type=MESH)
-        return src_f, src_b, to_right, to_left
-
+        to_right, to_left = copies(k)
+        last = k == rounds - 1
+
+        @pl.when(chip + shift < chips)
+        def _():
+            to_right.start()
+
+        @pl.when(chip >= shift)
+        def _():
+            to_left.start()
+
+        @pl.when(chip >= shift)
+        def _():
+            to_right.wait_recv()
+            got = got_f[k]
+            ex_f[...] += got
+            if not last:
+                tot_f[k + 1] = tot_f[k] + got
+
+        @pl.when(chip < shift)
+        def _():
+            if not last:
+                tot_f[k + 1] = tot_f[k]
+
+        @pl.when(chip + shift < chips)
+        def _():
+            to_left.wait_recv()
+            got = got_b[k]
+            ex_b[...] += got
+            if not last:
+                tot_b[k + 1] = tot_b[k] + got
+
+        @pl.when(chip + shift >= chips)
+        def _():
+            if not last:
+                tot_b[k + 1] = tot_b[k]
+
+    last_pair = on_chip(ex_f, fin_f, ex_b, fin_b, rounds + 1)
+    for copy in last_pair:
+        copy.start()
+    for copy in last_pair:
+        copy.wait_recv()
+
+    for mine in range(2):
+        rows = pl.ds(mine * half, half)
+        other = pl.ds((1 - mine) * half, half)
+
+        @pl.when(core == mine)
+        def _():
+            if mine == 0:
+                fwd_out[rows, :] = ex_f[...]
+                fwd_out[other, :] = fin_f[...]
+                bwd_out[rows, :] = ex_b[...] + peer_b[rows, :]
+                bwd_out[other, :] = fin_b[...] + peer_b[other, :]
+            else:
+                fwd_out[rows, :] = ex_f[...] + peer_f[rows, :]
+                fwd_out[other, :] = fin_f[...] + peer_f[other, :]
+                bwd_out[rows, :] = ex_b[...]
+                bwd_out[other, :] = fin_b[...]
+
+    for copy in first + last_pair:
+        copy.wait_send()
     for k in range(rounds):
         shift = 1 << k
-        src_f, src_b, to_right, to_left = copies(k)
-
-        @pl.when(me + shift < count)
-        def _():
-            to_right.start()
-
-        @pl.when(me >= shift)
-        def _():
-            to_left.start()
-
-        last = k == rounds - 1
-
-        @pl.when(me >= shift)
-        def _():
-            to_right.wait_recv()
-            got = fwd_got[k]
-            fwd_out[...] += got
-            if not last:
-                fwd_tot[k] = src_f[...] + got
-
-        @pl.when(me < shift)
-        def _():
-            if not last:
-                fwd_tot[k] = src_f[...]
-
-        @pl.when(me + shift < count)
-        def _():
-            to_left.wait_recv()
-            got = bwd_got[k]
-            bwd_out[...] += got
-            if not last:
-                bwd_tot[k] = src_b[...] + got
-
-        @pl.when(me + shift >= count)
-        def _():
-            if not last:
-                bwd_tot[k] = src_b[...]
-
-    for k in range(rounds):
-        shift = 1 << k
-        src_f, src_b, to_right, to_left = copies(k)
-
-        @pl.when(me + shift < count)
+        to_right, to_left = copies(k)
+
+        @pl.when(chip + shift < chips)
         def _():
             to_right.wait_send()
 
-        @pl.when(me >= shift)
+        @pl.when(chip >= shift)
         def _():
             to_left.wait_send()
+
+
+def exclusive_scans(forward_part, backward_part, axis):
+    count = lax.axis_size(axis)
+    chips = count // 2
+    rounds = max(1, (chips - 1).bit_length())
+    shape = forward_part.shape
+    fwd = forward_part.reshape(-1, shape[-1])
+    bwd = backward_part.reshape(-1, shape[-1])
+    rows, cols = fwd.shape
+    half = rows // 2
+    vmem = pl.BlockSpec(memory_space=pltpu.VMEM)
+    fwd_excl, bwd_excl = pl.pallas_call(
+        functools.partial(scan_kernel, chips, rounds, half),
+        out_shape=(jax.ShapeDtypeStruct(fwd.shape, fwd.dtype),) * 2,
+        in_specs=[vmem, vmem],
+        out_specs=(vmem, vmem),
+        scratch_shapes=[
+            pltpu.VMEM((rows, cols), jnp.float32),
+            pltpu.VMEM((rows, cols), jnp.float32),
+            pltpu.VMEM((rounds, half, cols), jnp.float32),
+            pltpu.VMEM((rounds, half, cols), jnp.float32),
+            pltpu.VMEM((rounds, half, cols), jnp.float32),
+            pltpu.VMEM((rounds, half, cols), jnp.float32),
+            pltpu.VMEM((half, cols), jnp.float32),
+            pltpu.VMEM((half, cols), jnp.float32),
+            pltpu.VMEM((half, cols), jnp.float32),
+            pltpu.VMEM((half, cols), jnp.float32),
+            pltpu.SemaphoreType.DMA((2, rounds + 2)),
+            pltpu.SemaphoreType.DMA((2, rounds + 2)),
+        ],
+        compiler_params=pltpu.CompilerParams(collective_id=0, has_side_effects=True,
+                                             vmem_limit_bytes=48 * 1024 * 1024),
+    )(fwd, bwd)
+    return fwd_excl.reshape(shape), bwd_excl.reshape(shape)
 
 
 def exchange_kernel(count, n_arrays, src_cut, dst_cut, *refs):
@@ -165,33 +249,6 @@
     )(*arrays)
 
 
-def exclusive_scans(forward_part, backward_part, axis):
-    count = lax.axis_size(axis)
-    rounds = max(1, (count - 1).bit_length())
-    shape = forward_part.shape
-    fwd = forward_part.reshape(-1, shape[-1])
-    bwd = backward_part.reshape(-1, shape[-1])
-    rows, cols = fwd.shape
-    vmem = pl.BlockSpec(memory_space=pltpu.VMEM)
-    fwd_excl, bwd_excl = pl.pallas_call(
-        functools.partial(scan_kernel, count, rounds),
-        out_shape=(jax.ShapeDtypeStruct(fwd.shape, fwd.dtype),) * 2,
-        in_specs=[vmem, vmem],
-        out_specs=(vmem, vmem),
-        scratch_shapes=[
-            pltpu.VMEM((rounds, rows, cols), jnp.float32),
-            pltpu.VMEM((rounds, rows, cols), jnp.float32),
-            pltpu.VMEM((rounds, rows, cols), jnp.float32),
-            pltpu.VMEM((rounds, rows, cols), jnp.float32),
-            pltpu.SemaphoreType.DMA((2, rounds)),
-            pltpu.SemaphoreType.DMA((2, rounds)),
-        ],
-        compiler_params=pltpu.CompilerParams(collective_id=0, has_side_effects=True,
-                                             vmem_limit_bytes=48 * 1024 * 1024),
-    )(fwd, bwd)
-    return fwd_excl.reshape(shape), bwd_excl.reshape(shape)
-
-
 def per_device(queries, key_rows, value_rows, grad_out):
     count = lax.axis_size("head")
     rows_in, width = queries.shape

time: 148 us -> 122 us (0.82)
  the two profiles are of different devices: /device:TPU:116 before, /device:TPU:1 now
where the time goes in v4:
time: 122 us; the launch traced here: 121 us
  Pallas kernels  104 us (85%)
  local copies, waits for them, and re-layouts  9.18 us (8%)
  matrix products  7.13 us (6%)
    pallas_call x2, Pallas kernels, exchange(): pl.pallas_call(functools.partial(exchange_kernel, count, n_arrays, src_cu...  54.5 us
    pallas_call x1, Pallas kernels, exclusive_scans(): pl.pallas_call(functools.partial(scan_kernel, chips, rounds, half), out_s...  49.6 us
    unnamed x16, local copies, waits for them, and re-layouts  5.77 us

profile of v4, /device:TPU:1, one launch (start us, length us, event | category | flops | bytes accessed | tf_op | source)
XLA Modules:
  0.0 121.2 jit_solution(595811845893379896)
XLA Ops:
  0.6 31.0 %shard_map.67 = (bf16[256,512]{1,0:T(8,128)(2,1)}, bf16[256,512]{1,0:T(8,128)(2,1)}, bf16[256,512]{1,0:T(8,128)(2,1)}, bf16[256,512]{1,0:T(8,128)(2,1)}) custom-call(bf16[32,4096]{1,0:T(8,128)(2,1)} %refs_0_.1, bf16[32,4096]{1,0:T(8,128)(2,1)} %refs_1_.1, bf16[32,4096]{1,0:T(8,128)(2,1)} %refs_2_.1, bf16[32,4096]{1,0:T(8,128)(2,1)} %refs_3_.1), custom_call_target="tpu_custom_call" | custom-call | tf_op jit(solution)/shard_map/pallas_call | solution.py:238
  31.7 0.0 copy-start.5
  31.7 1.1 reshape.45
  32.7 0.0 copy-done.5
  32.7 0.1 reshape.47
  32.8 0.3 fusion.43
  33.1 1.3 %fusion.12 = f32[2,4,128,128]{3,0,2,1:T(2,128)S(1)} fusion(f32[2,4,128,128]{3,2,1,0:T(8,128)S(1)} %get-tuple-element.16), kind=kOutput, calls=%fused_computation.19 | convolution fusion | flops 3145732 | bytes 1048576 | tf_op jit(solution)/shard_map/mn,nhab->mhab/dot_general | solution.py:283
  34.4 0.0 copy-start.2
  34.4 0.2 copy.28
  34.6 0.7 copy-done.2
  35.3 0.1 reshape.46
  35.4 0.0 copy-start.1
  35.4 0.2 copy.12
  35.6 0.7 copy-done.1
  36.4 0.1 reshape.49
  36.4 1.0 fusion.44
  37.5 49.6 %shard_map.68 = (f32[512,128]{1,0:T(8,128)S(1)}, f32[512,128]{1,0:T(8,128)S(1)}) custom-call(f32[512,128]{1,0:T(8,128)S(1)} %bitcast.39, f32[512,128]{1,0:T(8,128)S(1)} %bitcast.40), custom_call_target="tpu_custom_call" | custom-call | tf_op jit(solution)/shard_map/pallas_call | solution.py:166
  87.1 0.1 copy.14
  87.2 0.7 fusion.10
  87.9 0.2 copy.9
  88.1 0.3 fusion.4
  88.4 0.3 fusion.9
  88.7 0.0 copy-start
  88.7 0.2 copy.16
  88.9 0.7 copy.71
  89.6 0.1 copy-done
  89.7 1.4 %convolution_add_fusion = f32[2,4,128,128]{3,0,2,1:T(2,128)S(1)} fusion(f32[2,4,128,128]{3,2,1,0:T(8,128)S(1)} %copy-done, f32[4,128,128]{2,1,0:T(8,128)S(1)} %bitcast.41), kind=kOutput, calls=%fused_computation | convolution fusion | flops 3276804 | bytes 1310720 | tf_op jit(solution)/shard_map/mn,nhab->mhab/dot_general | solution.py:286
  91.1 0.7 convolution_multiply_fusion.2
  91.8 0.4 fusion.7
  92.2 0.2 copy.25
  92.4 0.6 fusion.15
  92.9 0.3 fusion.8
  93.2 0.2 copy.21
  93.4 0.9 copy_bitcast_fusion
  94.3 23.4 %shard_map.69 = (bf16[32,4096]{1,0:T(8,128)(2,1)}, bf16[32,4096]{1,0:T(8,128)(2,1)}, bf16[32,4096]{1,0:T(8,128)(2,1)}) custom-call(bf16[256,512]{1,0:T(8,128)(2,1)} %bitcast.43, bf16[256,512]{1,0:T(8,128)(2,1)} %get-tuple-element.20.refs_1_, bf16[256,512]{1,0:T(8,128)(2,1)} %get-tuple-element.19.refs_2_), custom_call_target="tpu_custom_call" | custom-call | tf_op jit(solution)/shard_map/pallas_call | solution.py:238
  117.8 0.0 copy-start.4
  117.8 1.7 %copy.75 = bf16[32,4096]{1,0:T(8,128)(2,1)} copy(bf16[32,4096]{1,0:T(8,128)(2,1)} %get-tuple-element.24) | data formatting | bytes 524288
  119.5 0.0 copy-done.4
  119.5 0.0 copy-start.3
  119.5 0.7 copy.76
  120.2 0.3 copy-done.3
  120.5 0.7 copy.77
  (2 shorter events, 0.0 us)
Async XLA Ops:
  31.7 1.1 copy-start.5
  34.4 1.0 copy-start.2
  35.4 1.0 copy-start.1
  88.7 1.0 copy-start
  117.8 1.7 %copy-start.4 = (bf16[32,4096]{1,0:T(8,128)(2,1)S(1)}, bf16[32,4096]{1,0:T(8,128)(2,1)}, u32[]{:S(2)}) copy-start(bf16[32,4096]{1,0:T(8,128)(2,1)} %get-tuple-element.25) | copy-start | bytes 786436
  119.5 1.0 copy-start.3

commit v5 on v4

--- a/solution.py
+++ b/solution.py
@@ -14,9 +14,17 @@
 MESH = pl.DeviceIdType.MESH
 
 
-def scan_kernel(chips, rounds, half, fwd_in, bwd_in, fwd_out, bwd_out,
+def _dot(a, b, ta=False, tb=False, precise=False):
+    dims = (((0 if ta else 1,), (1 if tb else 0,)), ((), ()))
+    return lax.dot_general(a, b, dims, preferred_element_type=jnp.float32,
+                           precision=lax.Precision.HIGHEST if precise else None)
+
+
+def core_kernel(chips, rounds, half, nblocks, heads, scale,
+                q_ref, k_ref, v_ref, d_ref, gq_ref, gk_ref, gv_ref,
+                fwd_in, bwd_in, kv_blk, g_blk, acc_q, acc_k, acc_v,
                 peer_f, peer_b, tot_f, tot_b, got_f, got_b, ex_f, ex_b, fin_f, fin_b,
-                send_sems, recv_sems):
+                fwd_out, bwd_out, send_sems, recv_sems):
     me = lax.axis_index("ctx")
     head = lax.axis_index("head")
     core = lax.rem(me, 2)
@@ -37,6 +45,26 @@
             pl.semaphore_signal(barrier, inc=1, device_id=(me - 2 * shift, head), device_id_type=MESH)
 
         peers = peers + (chip + shift < chips).astype(jnp.int32) + (chip >= shift).astype(jnp.int32)
+
+    blk = GROUP
+    dim = HEAD_DIM
+
+    def cut(ref, n, h):
+        return ref[n * blk:(n + 1) * blk, h * dim:(h + 1) * dim]
+
+    for h in range(heads):
+        rows = slice(h * dim, (h + 1) * dim)
+        for n in range(nblocks):
+            kv_blk[n, rows, :] = _dot(cut(v_ref, n, h), cut(k_ref, n, h), ta=True)
+            g_blk[n, rows, :] = _dot(cut(d_ref, n, h), cut(q_ref, n, h), ta=True)
+        kv_sum = kv_blk[0, rows, :]
+        g_sum = g_blk[0, rows, :]
+        for n in range(1, nblocks):
+            kv_sum = kv_sum + kv_blk[n, rows, :]
+            g_sum = g_sum + g_blk[n, rows, :]
+        fwd_in[rows, :] = kv_sum
+        bwd_in[rows, :] = g_sum
+
     pl.semaphore_wait(barrier, peers)
 
     def on_chip(src_f, dst_f, src_b, dst_b, slot):
@@ -52,6 +80,21 @@
     first = on_chip(fwd_in, peer_f, bwd_in, peer_b, 0)
     for copy in first:
         copy.start()
+
+    later = lax.broadcasted_iota(jnp.int32, (blk, blk), 0)
+    earlier = lax.broadcasted_iota(jnp.int32, (blk, blk), 1)
+    causal = later >= earlier
+    for h in range(heads):
+        for n in range(nblocks):
+            qb, kb, vb, db = (cut(r, n, h) for r in (q_ref, k_ref, v_ref, d_ref))
+            scores = jnp.where(causal, _dot(qb, kb, tb=True) * scale, 0.0).astype(jnp.bfloat16)
+            dscores = jnp.where(causal, _dot(db, vb, tb=True), 0.0).astype(jnp.bfloat16)
+            out_rows = slice(n * blk, (n + 1) * blk)
+            out_cols = slice(h * dim, (h + 1) * dim)
+            acc_q[out_rows, out_cols] = _dot(dscores, kb)
+            acc_k[out_rows, out_cols] = _dot(dscores, qb, ta=True)
+            acc_v[out_rows, out_cols] = _dot(scores, db, ta=True)
+
     for copy in first:
         copy.wait_recv()
 
@@ -138,6 +181,38 @@
                 bwd_out[rows, :] = ex_b[...]
                 bwd_out[other, :] = fin_b[...]
 
+    for h in range(heads):
+        rows = slice(h * dim, (h + 1) * dim)
+        kv_in = fwd_out[rows, :]
+        kv_states = []
+        for n in range(nblocks):
+            kv_states.append(kv_in)
+            if n + 1 < nblocks:
+                kv_in = kv_in + kv_blk[n, rows, :]
+        g_in = bwd_out[rows, :]
+        g_states = [None] * nblocks
+        for n in reversed(range(nblocks)):
+            g_states[n] = g_in
+            if n > 0:
+                g_in = g_in + g_blk[n, rows, :]
+        for n in range(nblocks):
+            out_rows = slice(n * blk, (n + 1) * blk)
+            out_cols = slice(h * dim, (h + 1) * dim)
+            kf = cut(k_ref, n, h).astype(jnp.float32)
+            vf = cut(v_ref, n, h).astype(jnp.float32)
+            df = cut(d_ref, n, h).astype(jnp.float32)
+            kv_s = kv_states[n]
+            g_s = g_states[n]
+            gq_ref[out_rows, out_cols] = (
+                scale * (acc_q[out_rows, out_cols] + _dot(df, kv_s, precise=True))
+            ).astype(gq_ref.dtype)
+            gk_ref[out_rows, out_cols] = (
+                scale * (acc_k[out_rows, out_cols] + _dot(vf, g_s, precise=True))
+            ).astype(gk_ref.dtype)
+            gv_ref[out_rows, out_cols] = (
+                acc_v[out_rows, out_cols] + scale * _dot(kf, g_s, tb=True, precise=True)
+            ).astype(gv_ref.dtype)
+
     for copy in first + last_pair:
         copy.wait_send()
     for k in range(rounds):
@@ -153,39 +228,49 @@
             to_left.wait_send()
 
 
-def exclusive_scans(forward_part, backward_part, axis):
-    count = lax.axis_size(axis)
+def core_math(q_all, k_all, v_all, d_all, scale):
+    count = lax.axis_size("ctx")
     chips = count // 2
     rounds = max(1, (chips - 1).bit_length())
-    shape = forward_part.shape
-    fwd = forward_part.reshape(-1, shape[-1])
-    bwd = backward_part.reshape(-1, shape[-1])
-    rows, cols = fwd.shape
+    tokens, width = q_all.shape
+    heads = width // HEAD_DIM
+    nblocks = tokens // GROUP
+    rows = heads * HEAD_DIM
     half = rows // 2
+    cols = HEAD_DIM
     vmem = pl.BlockSpec(memory_space=pltpu.VMEM)
-    fwd_excl, bwd_excl = pl.pallas_call(
-        functools.partial(scan_kernel, chips, rounds, half),
-        out_shape=(jax.ShapeDtypeStruct(fwd.shape, fwd.dtype),) * 2,
-        in_specs=[vmem, vmem],
-        out_specs=(vmem, vmem),
+    f32 = jnp.float32
+    return pl.pallas_call(
+        functools.partial(core_kernel, chips, rounds, half, nblocks, heads, scale),
+        out_shape=(jax.ShapeDtypeStruct(q_all.shape, q_all.dtype),) * 3,
+        in_specs=[vmem] * 4,
+        out_specs=(vmem,) * 3,
         scratch_shapes=[
-            pltpu.VMEM((rows, cols), jnp.float32),
-            pltpu.VMEM((rows, cols), jnp.float32),
-            pltpu.VMEM((rounds, half, cols), jnp.float32),
-            pltpu.VMEM((rounds, half, cols), jnp.float32),
-            pltpu.VMEM((rounds, half, cols), jnp.float32),
-            pltpu.VMEM((rounds, half, cols), jnp.float32),
-            pltpu.VMEM((half, cols), jnp.float32),
-            pltpu.VMEM((half, cols), jnp.float32),
-            pltpu.VMEM((half, cols), jnp.float32),
-            pltpu.VMEM((half, cols), jnp.float32),
+            pltpu.VMEM((rows, cols), f32),
+            pltpu.VMEM((rows, cols), f32),
+            pltpu.VMEM((nblocks, rows, cols), f32),
+            pltpu.VMEM((nblocks, rows, cols), f32),
+            pltpu.VMEM((tokens, width), f32),
+            pltpu.VMEM((tokens, width), f32),
+            pltpu.VMEM((tokens, width), f32),
+            pltpu.VMEM((rows, cols), f32),
+            pltpu.VMEM((rows, cols), f32),
+            pltpu.VMEM((rounds, half, cols), f32),
+            pltpu.VMEM((rounds, half, cols), f32),
+            pltpu.VMEM((rounds, half, cols), f32),
+            pltpu.VMEM((rounds, half, cols), f32),
+            pltpu.VMEM((half, cols), f32),
+            pltpu.VMEM((half, cols), f32),
+            pltpu.VMEM((half, cols), f32),
+            pltpu.VMEM((half, cols), f32),
+            pltpu.VMEM((rows, cols), f32),
+            pltpu.VMEM((rows, cols), f32),
             pltpu.SemaphoreType.DMA((2, rounds + 2)),
             pltpu.SemaphoreType.DMA((2, rounds + 2)),
         ],
         compiler_params=pltpu.CompilerParams(collective_id=0, has_side_effects=True,
                                              vmem_limit_bytes=48 * 1024 * 1024),
-    )(fwd, bwd)
-    return fwd_excl.reshape(shape), bwd_excl.reshape(shape)
+    )(q_all, k_all, v_all, d_all)
 
 
 def exchange_kernel(count, n_arrays, src_cut, dst_cut, *refs):
@@ -261,57 +346,8 @@
         1,
     )
     rows_here = q_all.shape[0]
-    heads_here = q_all.shape[1] // HEAD_DIM
     scale = (HEAD_DIM * rows_here * lax.axis_size("ctx")) ** (-0.5)
-    highest = lax.Precision.HIGHEST
-    block = GROUP
-    nblocks = rows_here // block
-    shape_four = (nblocks, block, heads_here, HEAD_DIM)
-    q_four = q_all.reshape(shape_four)
-    k_four = k_all.reshape(shape_four)
-    v_four = v_all.reshape(shape_four)
-    d_four = d_all.reshape(shape_four)
-    kv_blocks = jnp.einsum("ntha,nthb->nhab", v_four, k_four, preferred_element_type=jnp.float32)
-    g_blocks = jnp.einsum("ntha,nthb->nhab", d_four, q_four, preferred_element_type=jnp.float32)
-    kv_local = jnp.sum(kv_blocks, axis=0)
-    g_local = jnp.sum(g_blocks, axis=0)
-    kv_before, g_after = exclusive_scans(kv_local, g_local, "ctx")
-    row_ids = lax.broadcasted_iota(jnp.int32, (nblocks, nblocks), 0)
-    col_ids = lax.broadcasted_iota(jnp.int32, (nblocks, nblocks), 1)
-    strict_lower = (col_ids < row_ids).astype(jnp.float32)
-    strict_upper = (col_ids > row_ids).astype(jnp.float32)
-    kv_in = kv_before[None] + jnp.einsum(
-        "mn,nhab->mhab", strict_lower, kv_blocks, precision=highest
-    )
-    g_in = g_after[None] + jnp.einsum("mn,nhab->mhab", strict_upper, g_blocks, precision=highest)
-    later = lax.broadcasted_iota(jnp.int32, (block, block), 0)
-    earlier = lax.broadcasted_iota(jnp.int32, (block, block), 1)
-    causal = (later >= earlier).astype(jnp.float32)
-    scores = (
-        jnp.einsum("nthd,nshd->nhts", q_four, k_four, preferred_element_type=jnp.float32)
-        * (scale * causal)
-    ).astype(jnp.bfloat16)
-    dscores = (
-        jnp.einsum("nthd,nshd->nhts", d_four, v_four, preferred_element_type=jnp.float32) * causal
-    ).astype(jnp.bfloat16)
-    k_float = k_four.astype(jnp.float32)
-    v_float = v_four.astype(jnp.float32)
-    d_float = d_four.astype(jnp.float32)
-    grad_q = scale * (
-        jnp.einsum("nhts,nshd->nthd", dscores, k_four, preferred_element_type=jnp.float32)
-        + jnp.einsum("ntha,nhab->nthb", d_float, kv_in, precision=highest)
-    )
-    grad_k = scale * (
-        jnp.einsum("nhts,nthd->nshd", dscores, q_four, preferred_element_type=jnp.float32)
-        + jnp.einsum("ntha,nhab->nthb", v_float, g_in, precision=highest)
-    )
-    grad_v = jnp.einsum(
-        "nhts,nthd->nshd", scores, d_four, preferred_element_type=jnp.float32
-    ) + scale * jnp.einsum("nthb,nhab->ntha", k_float, g_in, precision=highest)
-    flat_shape = (rows_here, heads_here * HEAD_DIM)
-    grad_q = grad_q.reshape(flat_shape).astype(jnp.bfloat16)
-    grad_k = grad_k.reshape(flat_shape).astype(jnp.bfloat16)
-    grad_v = grad_v.reshape(flat_shape).astype(jnp.bfloat16)
+    grad_q, grad_k, grad_v = core_math(q_all, k_all, v_all, d_all, scale)
     result_q, result_k, result_v = exchange(
         (grad_q, grad_k, grad_v),
         (rows_in, width),

time: 122 us -> 116 us (0.951)
  matrix products: 7.13 us -> 0 us
  Pallas kernels: 104 us -> 106 us
    dot_general x11 -> x0, matrix products: 7.13 us -> none  [the longest x1 1.35 us: per_device(): jnp.einsum('mn,nhab->mhab', strict_upper, g_blocks, precision=highest)]
    unnamed x16 -> x21, local copies, waits for them, and re-layouts: 5.77 us -> 9.35 us
    pallas_call x1, Pallas kernels: 49.6 us -> 51.5 us  [core_math(): pl.pallas_call(functools.partial(core_kernel, chips, rounds, half, nblock...]
    reshape x6 -> x0, local copies, waits for them, and re-layouts: 1.63 us -> none  [the longest x2 1.25 us: per_device(): k_four = k_all.reshape(shape_four)]
    convert_element_type x4 -> x0, local copies, waits for them, and re-layouts: 1.44 us -> none  [the longest x2 1.05 us: per_device(): grad_v = grad_v.reshape(flat_shape).astype(jnp.bfloat16)]
where the time goes in v5:
time: 116 us
  Pallas kernels  106 us (91%)
  local copies, waits for them, and re-layouts  9.35 us (8%)
    pallas_call x2, Pallas kernels, exchange(): pl.pallas_call(functools.partial(exchange_kernel, count, n_arrays, src_cu...  54.4 us
    pallas_call x1, Pallas kernels, core_math(): pl.pallas_call(functools.partial(core_kernel, chips, rounds, half, nblock...  51.5 us
    unnamed x21, local copies, waits for them, and re-layouts  9.35 us

profile of v5, /device:TPU:1, one launch (start us, length us, event | category | flops | bytes accessed | tf_op | source)
XLA Modules:
  0.0 115.9 jit_solution(11427391243086878849)
XLA Ops:
  0.6 31.0 %shard_map.67 = (bf16[256,512]{1,0:T(8,128)(2,1)}, bf16[256,512]{1,0:T(8,128)(2,1)}, bf16[256,512]{1,0:T(8,128)(2,1)}, bf16[256,512]{1,0:T(8,128)(2,1)}) custom-call(bf16[32,4096]{1,0:T(8,128)(2,1)} %refs_0_.1, bf16[32,4096]{1,0:T(8,128)(2,1)} %refs_1_.1, bf16[32,4096]{1,0:T(8,128)(2,1)} %refs_2_.1, bf16[32,4096]{1,0:T(8,128)(2,1)} %refs_3_.1), custom_call_target="tpu_custom_call" | custom-call | tf_op jit(solution)/shard_map/pallas_call | solution.py:323
  31.7 0.0 copy-start.3
  31.7 0.9 copy-done.3
  32.6 0.0 copy-start.4
  32.6 0.9 copy-done.4
  33.6 0.0 copy-start.5
  33.6 0.9 copy-done.5
  34.5 0.0 copy-start.6
  34.5 0.9 copy-done.6
  35.5 51.5 %shard_map.68 = (bf16[256,512]{1,0:T(8,128)(2,1)S(1)}, bf16[256,512]{1,0:T(8,128)(2,1)S(1)}, bf16[256,512]{1,0:T(8,128)(2,1)S(1)}) custom-call(bf16[256,512]{1,0:T(8,128)(2,1)S(1)} %copy-done.3, bf16[256,512]{1,0:T(8,128)(2,1)S(1)} %copy-done.4, bf16[256,512]{1,0:T(8,128)(2,1)S(1)} %copy-done.5, bf16[256,512]{1,0:T(8,128)(2,1)S(1)} %copy-done.6), custom_call_target="tpu_custom_call" | custom-call | tf_op jit(solution)/shard_map/pallas_call | solution.py:243
  87.0 0.0 copy-start
  87.0 0.7 copy-done
  87.7 0.0 copy-start.1
  87.7 0.7 copy-done.1
  88.4 0.0 copy-start.2
  88.4 0.7 copy-done.2
  89.1 23.3 %shard_map.69 = (bf16[32,4096]{1,0:T(8,128)(2,1)}, bf16[32,4096]{1,0:T(8,128)(2,1)}, bf16[32,4096]{1,0:T(8,128)(2,1)}) custom-call(bf16[256,512]{1,0:T(8,128)(2,1)} %copy-done, bf16[256,512]{1,0:T(8,128)(2,1)} %copy-done.1, bf16[256,512]{1,0:T(8,128)(2,1)} %copy-done.2), custom_call_target="tpu_custom_call" | custom-call | tf_op jit(solution)/shard_map/pallas_call | solution.py:323
  112.4 0.0 copy-start.8
  112.4 1.7 %copy.10 = bf16[32,4096]{1,0:T(8,128)(2,1)} copy(bf16[32,4096]{1,0:T(8,128)(2,1)} %get-tuple-element.20) | data formatting | bytes 524288
  114.2 0.0 copy-done.8
  114.2 0.0 copy-start.7
  114.2 0.7 copy.11
  114.9 0.3 copy-done.7
  115.2 0.7 copy.12
Async XLA Ops:
  31.7 1.0 copy-start.3
  32.6 0.9 copy-start.4
  33.6 0.9 copy-start.5
  34.5 0.9 copy-start.6
  87.0 0.7 copy-start
  87.7 0.7 copy-start.1
  88.4 0.7 copy-start.2
  112.4 1.7 %copy-start.8 = (bf16[32,4096]{1,0:T(8,128)(2,1)S(1)}, bf16[32,4096]{1,0:T(8,128)(2,1)}, u32[]{:S(2)}) copy-start(bf16[32,4096]{1,0:T(8,128)(2,1)} %get-tuple-element.21) | copy-start | bytes 786436
  114.2 1.0 copy-start.7

commit v6 on v5

--- a/solution.py
+++ b/solution.py
@@ -20,31 +20,45 @@
                            precision=lax.Precision.HIGHEST if precise else None)
 
 
-def core_kernel(chips, rounds, half, nblocks, heads, scale,
+def core_kernel(plane, planes, rounds, half, nblocks, heads, scale,
                 q_ref, k_ref, v_ref, d_ref, gq_ref, gk_ref, gv_ref,
                 fwd_in, bwd_in, kv_blk, g_blk, acc_q, acc_k, acc_v,
-                peer_f, peer_b, tot_f, tot_b, got_f, got_b, ex_f, ex_b, fin_f, fin_b,
-                fwd_out, bwd_out, send_sems, recv_sems):
+                peer_f, peer_b, th_f, th_b, in_b1, pre, tz_f, tz_b, got_f, got_b,
+                ez_f, ez_b, out_d, in_d, res_f, res_b, fin_f, fin_b,
+                fwd_out, bwd_out, sems):
     me = lax.axis_index("ctx")
     head = lax.axis_index("head")
     core = lax.rem(me, 2)
     chip = me // 2
+    x = lax.rem(chip, plane)
+    z = chip // plane
     partner = me + 1 - 2 * core
+    qr = half // plane
+
+    def dev(xp, zp):
+        return ((zp * plane + xp) * 2 + core, head)
+
     barrier = pltpu.get_barrier_semaphore()
     pl.semaphore_signal(barrier, inc=1, device_id=(partner, head), device_id_type=MESH)
     peers = 1
+    for xp in range(plane):
+        @pl.when(x != xp)
+        def _():
+            pl.semaphore_signal(barrier, inc=1, device_id=dev(xp, z), device_id_type=MESH)
+
+        peers = peers + (x != xp).astype(jnp.int32)
     for k in range(rounds):
         shift = 1 << k
 
-        @pl.when(chip + shift < chips)
-        def _():
-            pl.semaphore_signal(barrier, inc=1, device_id=(me + 2 * shift, head), device_id_type=MESH)
-
-        @pl.when(chip >= shift)
-        def _():
-            pl.semaphore_signal(barrier, inc=1, device_id=(me - 2 * shift, head), device_id_type=MESH)
-
-        peers = peers + (chip + shift < chips).astype(jnp.int32) + (chip >= shift).astype(jnp.int32)
+        @pl.when(z + shift < planes)
+        def _():
+            pl.semaphore_signal(barrier, inc=1, device_id=dev(x, z + shift), device_id_type=MESH)
+
+        @pl.when(z >= shift)
+        def _():
+            pl.semaphore_signal(barrier, inc=1, device_id=dev(x, z - shift), device_id_type=MESH)
+
+        peers = peers + (z + shift < planes).astype(jnp.int32) + (z >= shift).astype(jnp.int32)
 
     blk = GROUP
     dim = HEAD_DIM
@@ -67,17 +81,13 @@
 
     pl.semaphore_wait(barrier, peers)
 
-    def on_chip(src_f, dst_f, src_b, dst_b, slot):
-        return (
-            pltpu.make_async_remote_copy(
-                src_ref=src_f, dst_ref=dst_f, send_sem=send_sems.at[0, slot],
-                recv_sem=recv_sems.at[0, slot], device_id=(partner, head), device_id_type=MESH),
-            pltpu.make_async_remote_copy(
-                src_ref=src_b, dst_ref=dst_b, send_sem=send_sems.at[1, slot],
-                recv_sem=recv_sems.at[1, slot], device_id=(partner, head), device_id_type=MESH),
-        )
-
-    first = on_chip(fwd_in, peer_f, bwd_in, peer_b, 0)
+    def remote(src, dst, sem_send, sem_recv, device):
+        return pltpu.make_async_remote_copy(
+            src_ref=src, dst_ref=dst, send_sem=sem_send, recv_sem=sem_recv,
+            device_id=device, device_id_type=MESH)
+
+    first = (remote(fwd_in, peer_f, sems.at[0, 0, 0, 0], sems.at[1, 0, 0, 0], (partner, head)),
+             remote(bwd_in, peer_b, sems.at[0, 0, 1, 0], sems.at[1, 0, 1, 0], (partner, head)))
     for copy in first:
         copy.start()
 
@@ -103,62 +113,121 @@
 
         @pl.when(core == mine)
         def _():
-            tot_f[0] = fwd_in[rows, :] + peer_f[rows, :]
-            tot_b[0] = bwd_in[rows, :] + peer_b[rows, :]
-
-    ex_f[...] = jnp.zeros_like(ex_f)
-    ex_b[...] = jnp.zeros_like(ex_b)
-
-    def copies(k):
+            th_f[...] = fwd_in[rows, :] + peer_f[rows, :]
+            th_b[...] = bwd_in[rows, :] + peer_b[rows, :]
+
+    halves = (th_f, th_b)
+
+    def scatter(s, xp):
+        return remote(halves[s].at[pl.ds(xp * qr, qr)], in_b1.at[s, x],
+                      sems.at[0, 2, s, xp], sems.at[1, 2, s, x], dev(xp, z))
+
+    def scatter_in(s, xp):
+        return remote(halves[s].at[pl.ds(xp * qr, qr)], in_b1.at[s, xp],
+                      sems.at[0, 2, s, xp], sems.at[1, 2, s, xp], dev(xp, z))
+
+    for s in range(2):
+        for xp in range(plane):
+            @pl.when(x != xp)
+            def _():
+                scatter(s, xp).start()
+    for s in range(2):
+        in_b1[s, x] = halves[s][pl.ds(x * qr, qr), :]
+    for s in range(2):
+        for xp in range(plane):
+            @pl.when(x != xp)
+            def _():
+                scatter_in(s, xp).wait_recv()
+
+    run = jnp.zeros((qr, HEAD_DIM), jnp.float32)
+    for xp in range(plane):
+        pre[0, xp] = run
+        run = run + in_b1[0, xp]
+    tz_f[0] = run
+    run = jnp.zeros((qr, HEAD_DIM), jnp.float32)
+    for xp in reversed(range(plane)):
+        pre[1, xp] = run
+        run = run + in_b1[1, xp]
+    tz_b[0] = run
+
+    ez_f[...] = jnp.zeros_like(ez_f)
+    ez_b[...] = jnp.zeros_like(ez_b)
+
+    def z_copies(k):
         shift = 1 << k
-        to_right = pltpu.make_async_remote_copy(
-            src_ref=tot_f.at[k], dst_ref=got_f.at[k], send_sem=send_sems.at[0, k + 1],
-            recv_sem=recv_sems.at[0, k + 1], device_id=(me + 2 * shift, head), device_id_type=MESH)
-        to_left = pltpu.make_async_remote_copy(
-            src_ref=tot_b.at[k], dst_ref=got_b.at[k], send_sem=send_sems.at[1, k + 1],
-            recv_sem=recv_sems.at[1, k + 1], device_id=(me - 2 * shift, head), device_id_type=MESH)
-        return to_right, to_left
+        up = remote(tz_f.at[k], got_f.at[k], sems.at[0, 3, 0, k], sems.at[1, 3, 0, k], dev(x, z + shift))
+        down = remote(tz_b.at[k], got_b.at[k], sems.at[0, 3, 1, k], sems.at[1, 3, 1, k], dev(x, z - shift))
+        return up, down
 
     for k in range(rounds):
         shift = 1 << k
-        to_right, to_left = copies(k)
+        up, down = z_copies(k)
         last = k == rounds - 1
 
-        @pl.when(chip + shift < chips)
-        def _():
-            to_right.start()
-
-        @pl.when(chip >= shift)
-        def _():
-            to_left.start()
-
-        @pl.when(chip >= shift)
-        def _():
-            to_right.wait_recv()
+        @pl.when(z + shift < planes)
+        def _():
+            up.start()
+
+        @pl.when(z >= shift)
+        def _():
+            down.start()
+
+        @pl.when(z >= shift)
+        def _():
+            up.wait_recv()
             got = got_f[k]
-            ex_f[...] += got
+            ez_f[...] += got
             if not last:
-                tot_f[k + 1] = tot_f[k] + got
-
-        @pl.when(chip < shift)
+                tz_f[k + 1] = tz_f[k] + got
+
+        @pl.when(z < shift)
         def _():
             if not last:
-                tot_f[k + 1] = tot_f[k]
-
-        @pl.when(chip + shift < chips)
-        def _():
-            to_left.wait_recv()
+                tz_f[k + 1] = tz_f[k]
+
+        @pl.when(z + shift < planes)
+        def _():
+            down.wait_recv()
             got = got_b[k]
-            ex_b[...] += got
+            ez_b[...] += got
             if not last:
-                tot_b[k + 1] = tot_b[k] + got
-
-        @pl.when(chip + shift >= chips)
+                tz_b[k + 1] = tz_b[k] + got
+
+        @pl.when(z + shift >= planes)
         def _():
             if not last:
-                tot_b[k + 1] = tot_b[k]
-
-    last_pair = on_chip(ex_f, fin_f, ex_b, fin_b, rounds + 1)
+                tz_b[k + 1] = tz_b[k]
+
+    zs = (ez_f, ez_b)
+    for s in range(2):
+        for xp in range(plane):
+            out_d[s, xp] = zs[s][...] + pre[s, xp]
+
+    def gather(s, xp):
+        return remote(out_d.at[s, xp], in_d.at[s, x],
+                      sems.at[0, 4, s, xp], sems.at[1, 4, s, x], dev(xp, z))
+
+    def gather_in(s, xp):
+        return remote(out_d.at[s, xp], in_d.at[s, xp],
+                      sems.at[0, 4, s, xp], sems.at[1, 4, s, xp], dev(xp, z))
+
+    for s in range(2):
+        for xp in range(plane):
+            @pl.when(x != xp)
+            def _():
+                gather(s, xp).start()
+    results = (res_f, res_b)
+    for s in range(2):
+        results[s][pl.ds(x * qr, qr), :] = out_d[s, x]
+    for s in range(2):
+        for xp in range(plane):
+            @pl.when(x != xp)
+            def _():
+                gather_in(s, xp).wait_recv()
+                results[s][xp * qr:(xp + 1) * qr, :] = in_d[s, xp]
+
+    last_pair = (remote(res_f, fin_f, sems.at[0, 1, 0, 0], sems.at[1, 1, 0, 0], (partner, head)),
+                 remote(res_b, fin_b, sems.at[0, 1, 1, 0], sems.at[1, 1, 1, 0], (partner, head)))
     for copy in last_pair:
         copy.start()
     for copy in last_pair:
@@ -171,14 +240,14 @@
         @pl.when(core == mine)
         def _():
             if mine == 0:
-                fwd_out[rows, :] = ex_f[...]
+                fwd_out[rows, :] = res_f[...]
                 fwd_out[other, :] = fin_f[...]
-                bwd_out[rows, :] = ex_b[...] + peer_b[rows, :]
+                bwd_out[rows, :] = res_b[...] + peer_b[rows, :]
                 bwd_out[other, :] = fin_b[...] + peer_b[other, :]
             else:
-                fwd_out[rows, :] = ex_f[...] + peer_f[rows, :]
+                fwd_out[rows, :] = res_f[...] + peer_f[rows, :]
                 fwd_out[other, :] = fin_f[...] + peer_f[other, :]
-                bwd_out[rows, :] = ex_b[...]
+                bwd_out[rows, :] = res_b[...]
                 bwd_out[other, :] = fin_b[...]
 
     for h in range(heads):
@@ -215,33 +284,45 @@
 
     for copy in first + last_pair:
         copy.wait_send()
+    for s in range(2):
+        for xp in range(plane):
+            @pl.when(x != xp)
+            def _():
+                scatter(s, xp).wait_send()
+                gather(s, xp).wait_send()
     for k in range(rounds):
         shift = 1 << k
-        to_right, to_left = copies(k)
-
-        @pl.when(chip + shift < chips)
-        def _():
-            to_right.wait_send()
-
-        @pl.when(chip >= shift)
-        def _():
-            to_left.wait_send()
+        up, down = z_copies(k)
+
+        @pl.when(z + shift < planes)
+        def _():
+            up.wait_send()
+
+        @pl.when(z >= shift)
+        def _():
+            down.wait_send()
+
+
+PLANE = 4
 
 
 def core_math(q_all, k_all, v_all, d_all, scale):
     count = lax.axis_size("ctx")
     chips = count // 2
-    rounds = max(1, (chips - 1).bit_length())
+    plane = PLANE if chips % PLANE == 0 else 1
+    planes = chips // plane
+    rounds = max(1, (planes - 1).bit_length())
     tokens, width = q_all.shape
     heads = width // HEAD_DIM
     nblocks = tokens // GROUP
     rows = heads * HEAD_DIM
     half = rows // 2
+    qr = half // plane
     cols = HEAD_DIM
     vmem = pl.BlockSpec(memory_space=pltpu.VMEM)
     f32 = jnp.float32
     return pl.pallas_call(
-        functools.partial(core_kernel, chips, rounds, half, nblocks, heads, scale),
+        functools.partial(core_kernel, plane, planes, rounds, half, nblocks, heads, scale),
         out_shape=(jax.ShapeDtypeStruct(q_all.shape, q_all.dtype),) * 3,
         in_specs=[vmem] * 4,
         out_specs=(vmem,) * 3,
@@ -255,18 +336,25 @@
             pltpu.VMEM((tokens, width), f32),
             pltpu.VMEM((rows, cols), f32),
             pltpu.VMEM((rows, cols), f32),
-            pltpu.VMEM((rounds, half, cols), f32),
-            pltpu.VMEM((rounds, half, cols), f32),
-            pltpu.VMEM((rounds, half, cols), f32),
-            pltpu.VMEM((rounds, half, cols), f32),
-            pltpu.VMEM((half, cols), f32),
-            pltpu.VMEM((half, cols), f32),
-            pltpu.VMEM((half, cols), f32),
-            pltpu.VMEM((half, cols), f32),
-            pltpu.VMEM((rows, cols), f32),
-            pltpu.VMEM((rows, cols), f32),
-            pltpu.SemaphoreType.DMA((2, rounds + 2)),
-            pltpu.SemaphoreType.DMA((2, rounds + 2)),
+            pltpu.VMEM((half, cols), f32),
+            pltpu.VMEM((half, cols), f32),
+            pltpu.VMEM((2, plane, qr, cols), f32),
+            pltpu.VMEM((2, plane, qr, cols), f32),
+            pltpu.VMEM((rounds, qr, cols), f32),
+            pltpu.VMEM((rounds, qr, cols), f32),
+            pltpu.VMEM((rounds, qr, cols), f32),
+            pltpu.VMEM((rounds, qr, cols), f32),
+            pltpu.VMEM((qr, cols), f32),
+            pltpu.VMEM((qr, cols), f32),
+            pltpu.VMEM((2, plane, qr, cols), f32),
+            pltpu.VMEM((2, plane, qr, cols), f32),
+            pltpu.VMEM((half, cols), f32),
+            pltpu.VMEM((half, cols), f32),
+            pltpu.VMEM((half, cols), f32),
+            pltpu.VMEM((half, cols), f32),
+            pltpu.VMEM((rows, cols), f32),
+            pltpu.VMEM((rows, cols), f32),
+            pltpu.SemaphoreType.DMA((2, 5, 2, max(plane, rounds))),
         ],
         compiler_params=pltpu.CompilerParams(collective_id=0, has_side_effects=True,
                                              vmem_limit_bytes=48 * 1024 * 1024),
@@ -318,6 +406,8 @@
 
 def exchange(arrays, out_shape, src_cut, dst_cut, collective_id):
     count = lax.axis_size("head")
+    if count == 1:
+        return tuple(arrays)
     n_arrays = len(arrays)
     anywhere = pl.BlockSpec(memory_space=pl.ANY)
     return pl.pallas_call(

time: 116 us -> 106 us (0.914)
  Pallas kernels: 106 us -> 95.6 us
    pallas_call x1, Pallas kernels: 51.5 us -> 41.2 us  [core_math(): pl.pallas_call(functools.partial(core_kernel, plane, planes, rounds, half...]
where the time goes in v6:
time: 106 us
  Pallas kernels  95.6 us (90%)
  local copies, waits for them, and re-layouts  9.35 us (9%)
    pallas_call x2, Pallas kernels, exchange(): pl.pallas_call(functools.partial(exchange_kernel, count, n_arrays, src_cu...  54.4 us
    pallas_call x1, Pallas kernels, core_math(): pl.pallas_call(functools.partial(core_kernel, plane, planes, rounds, half...  41.2 us
    unnamed x21, local copies, waits for them, and re-layouts  9.35 us

profile of v6, /device:TPU:1, one launch (start us, length us, event | category | flops | bytes accessed | tf_op | source)
XLA Modules:
  0.0 105.7 jit_solution(7739268412308945849)
XLA Ops:
  0.6 31.0 %shard_map.67 = (bf16[256,512]{1,0:T(8,128)(2,1)}, bf16[256,512]{1,0:T(8,128)(2,1)}, bf16[256,512]{1,0:T(8,128)(2,1)}, bf16[256,512]{1,0:T(8,128)(2,1)}) custom-call(bf16[32,4096]{1,0:T(8,128)(2,1)} %refs_0_.1, bf16[32,4096]{1,0:T(8,128)(2,1)} %refs_1_.1, bf16[32,4096]{1,0:T(8,128)(2,1)} %refs_2_.1, bf16[32,4096]{1,0:T(8,128)(2,1)} %refs_3_.1), custom_call_target="tpu_custom_call" | custom-call | tf_op jit(solution)/shard_map/pallas_call | solution.py:413
  31.7 0.0 copy-start.3
  31.7 0.9 copy-done.3
  32.6 0.0 copy-start.4
  32.6 0.9 copy-done.4
  33.6 0.0 copy-start.5
  33.6 0.9 copy-done.5
  34.5 0.0 copy-start.6
  34.5 0.9 copy-done.6
  35.5 41.2 %shard_map.68 = (bf16[256,512]{1,0:T(8,128)(2,1)S(1)}, bf16[256,512]{1,0:T(8,128)(2,1)S(1)}, bf16[256,512]{1,0:T(8,128)(2,1)S(1)}) custom-call(bf16[256,512]{1,0:T(8,128)(2,1)S(1)} %copy-done.3, bf16[256,512]{1,0:T(8,128)(2,1)S(1)} %copy-done.4, bf16[256,512]{1,0:T(8,128)(2,1)S(1)} %copy-done.5, bf16[256,512]{1,0:T(8,128)(2,1)S(1)} %copy-done.6), custom_call_target="tpu_custom_call" | custom-call | tf_op jit(solution)/shard_map/pallas_call | solution.py:324
  76.7 0.0 copy-start
  76.7 0.7 copy-done
  77.4 0.0 copy-start.1
  77.4 0.7 copy-done.1
  78.1 0.0 copy-start.2
  78.1 0.7 copy-done.2
  78.8 23.4 %shard_map.69 = (bf16[32,4096]{1,0:T(8,128)(2,1)}, bf16[32,4096]{1,0:T(8,128)(2,1)}, bf16[32,4096]{1,0:T(8,128)(2,1)}) custom-call(bf16[256,512]{1,0:T(8,128)(2,1)} %copy-done, bf16[256,512]{1,0:T(8,128)(2,1)} %copy-done.1, bf16[256,512]{1,0:T(8,128)(2,1)} %copy-done.2), custom_call_target="tpu_custom_call" | custom-call | tf_op jit(solution)/shard_map/pallas_call | solution.py:413
  102.2 0.0 copy-start.8
  102.2 1.7 %copy.10 = bf16[32,4096]{1,0:T(8,128)(2,1)} copy(bf16[32,4096]{1,0:T(8,128)(2,1)} %get-tuple-element.20) | data formatting | bytes 524288
  103.9 0.0 copy-done.8
  103.9 0.0 copy-start.7
  103.9 0.7 copy.11
  104.6 0.3 copy-done.7
  105.0 0.7 copy.12
Async XLA Ops:
  31.7 1.0 copy-start.3
  32.6 0.9 copy-start.4
  33.6 0.9 copy-start.5
  34.5 0.9 copy-start.6
  76.7 0.7 copy-start
  77.4 0.7 copy-start.1
  78.1 0.7 copy-start.2
  102.2 1.7 %copy-start.8 = (bf16[32,4096]{1,0:T(8,128)(2,1)S(1)}, bf16[32,4096]{1,0:T(8,128)(2,1)}, u32[]{:S(2)}) copy-start(bf16[32,4096]{1,0:T(8,128)(2,1)} %get-tuple-element.21) | copy-start | bytes 786436
  103.9 1.0 copy-start.7

commit v7 on v6

--- a/solution.py
+++ b/solution.py
@@ -21,7 +21,8 @@
 
 
 def core_kernel(plane, planes, rounds, half, nblocks, heads, scale,
-                q_ref, k_ref, v_ref, d_ref, gq_ref, gk_ref, gv_ref,
+                q_hbm, k_hbm, v_hbm, d_hbm, gq_hbm, gk_hbm, gv_hbm,
+                q_ref, k_ref, v_ref, d_ref, gq_ref, gk_ref, gv_ref, io_sems,
                 fwd_in, bwd_in, kv_blk, g_blk, acc_q, acc_k, acc_v,
                 peer_f, peer_b, th_f, th_b, in_b1, pre, tz_f, tz_b, got_f, got_b,
                 ez_f, ez_b, out_d, in_d, res_f, res_b, fin_f, fin_b,
@@ -59,6 +60,13 @@
             pl.semaphore_signal(barrier, inc=1, device_id=dev(x, z - shift), device_id_type=MESH)
 
         peers = peers + (z + shift < planes).astype(jnp.int32) + (z >= shift).astype(jnp.int32)
+
+    loads = [pltpu.make_async_copy(hbm, ref, io_sems.at[i])
+             for i, (hbm, ref) in enumerate(zip((q_hbm, k_hbm, v_hbm, d_hbm), (q_ref, k_ref, v_ref, d_ref)))]
+    for copy in loads:
+        copy.start()
+    for copy in loads:
+        copy.wait()
 
     blk = GROUP
     dim = HEAD_DIM
@@ -282,6 +290,10 @@
                 acc_v[out_rows, out_cols] + scale * _dot(kf, g_s, tb=True, precise=True)
             ).astype(gv_ref.dtype)
 
+    stores = [pltpu.make_async_copy(ref, hbm, io_sems.at[4 + i])
+              for i, (ref, hbm) in enumerate(zip((gq_ref, gk_ref, gv_ref), (gq_hbm, gk_hbm, gv_hbm)))]
+    for copy in stores:
+        copy.start()
     for copy in first + last_pair:
         copy.wait_send()
     for s in range(2):
@@ -301,9 +313,12 @@
         @pl.when(z >= shift)
         def _():
             down.wait_send()
+    for copy in stores:
+        copy.wait()
 
 
 PLANE = 4
+VMEM_ALL = 67043328
 
 
 def core_math(q_all, k_all, v_all, d_all, scale):
@@ -319,14 +334,16 @@
     half = rows // 2
     qr = half // plane
     cols = HEAD_DIM
-    vmem = pl.BlockSpec(memory_space=pltpu.VMEM)
+    anywhere = pl.BlockSpec(memory_space=pl.ANY)
     f32 = jnp.float32
     return pl.pallas_call(
         functools.partial(core_kernel, plane, planes, rounds, half, nblocks, heads, scale),
         out_shape=(jax.ShapeDtypeStruct(q_all.shape, q_all.dtype),) * 3,
-        in_specs=[vmem] * 4,
-        out_specs=(vmem,) * 3,
+        in_specs=[anywhere] * 4,
+        out_specs=(anywhere,) * 3,
         scratch_shapes=[
+            *[pltpu.VMEM((tokens, width), q_all.dtype) for _ in range(7)],
+            pltpu.SemaphoreType.DMA((7,)),
             pltpu.VMEM((rows, cols), f32),
             pltpu.VMEM((rows, cols), f32),
             pltpu.VMEM((nblocks, rows, cols), f32),
@@ -357,7 +374,7 @@
             pltpu.SemaphoreType.DMA((2, 5, 2, max(plane, rounds))),
         ],
         compiler_params=pltpu.CompilerParams(collective_id=0, has_side_effects=True,
-                                             vmem_limit_bytes=48 * 1024 * 1024),
+                                             vmem_limit_bytes=VMEM_ALL),
     )(q_all, k_all, v_all, d_all)
 
 
@@ -404,23 +421,25 @@
                 copy.wait_recv()
 
 
-def exchange(arrays, out_shape, src_cut, dst_cut, collective_id):
+def exchange(arrays, out_shape, src_cut, dst_cut, collective_id, in_space, out_space):
     count = lax.axis_size("head")
     if count == 1:
         return tuple(arrays)
     n_arrays = len(arrays)
-    anywhere = pl.BlockSpec(memory_space=pl.ANY)
+    in_spec = pl.BlockSpec(memory_space=in_space)
+    out_spec = pl.BlockSpec(memory_space=out_space)
     return pl.pallas_call(
         functools.partial(exchange_kernel, count, n_arrays, src_cut, dst_cut),
         out_shape=tuple(jax.ShapeDtypeStruct(out_shape, arrays[0].dtype) for _ in arrays),
-        in_specs=[anywhere] * n_arrays,
-        out_specs=tuple(anywhere for _ in arrays),
+        in_specs=[in_spec] * n_arrays,
+        out_specs=tuple(out_spec for _ in arrays),
         scratch_shapes=[
             pltpu.SemaphoreType.DMA((n_arrays, count)),
             pltpu.SemaphoreType.DMA((n_arrays, count)),
             pltpu.SemaphoreType.DMA((n_arrays,)),
         ],
-        compiler_params=pltpu.CompilerParams(collective_id=collective_id, has_side_effects=True),
+        compiler_params=pltpu.CompilerParams(collective_id=collective_id, has_side_effects=True,
+                                             vmem_limit_bytes=VMEM_ALL),
     )(*arrays)
 
 
@@ -434,6 +453,8 @@
         lambda ref, j: ref.at[:, pl.ds(j * cols, cols)],
         lambda ref, j: ref.at[pl.ds(j * rows_in, rows_in), :],
         1,
+        pl.ANY,
+        pl.ANY,
     )
     rows_here = q_all.shape[0]
     scale = (HEAD_DIM * rows_here * lax.axis_size("ctx")) ** (-0.5)
@@ -444,6 +465,8 @@
         lambda ref, j: ref.at[pl.ds(j * rows_in, rows_in), :],
         lambda ref, j: ref.at[:, pl.ds(j * cols, cols)],
         2,
+        pl.ANY,
+        pl.ANY,
     )
     return (result_q, result_k, result_v)
 

time: 106 us -> 101 us (0.953)
  local copies, waits for them, and re-layouts: 9.35 us -> 3.46 us
    unnamed x21 -> x7, local copies, waits for them, and re-layouts: 9.35 us -> 3.46 us
where the time goes in v7:
time: 101 us
  Pallas kernels  96.4 us (95%)
  local copies, waits for them, and re-layouts  3.46 us (3%)
    pallas_call x2, Pallas kernels, exchange(): pl.pallas_call(functools.partial(exchange_kernel, count, n_arrays, src_cu...  54.4 us
    pallas_call x1, Pallas kernels, core_math(): pl.pallas_call(functools.partial(core_kernel, plane, planes, rounds, half...  42 us
    unnamed x7, local copies, waits for them, and re-layouts  3.46 us

profile of v7, /device:TPU:1, one launch (start us, length us, event | category | flops | bytes accessed | tf_op | source)
XLA Modules:
  0.0 100.5 jit_solution(7052903337193322377)
XLA Ops:
  0.6 31.0 %shard_map.67 = (bf16[256,512]{1,0:T(8,128)(2,1)}, bf16[256,512]{1,0:T(8,128)(2,1)}, bf16[256,512]{1,0:T(8,128)(2,1)}, bf16[256,512]{1,0:T(8,128)(2,1)}) custom-call(bf16[32,4096]{1,0:T(8,128)(2,1)} %refs_0_.1, bf16[32,4096]{1,0:T(8,128)(2,1)} %refs_1_.1, bf16[32,4096]{1,0:T(8,128)(2,1)} %refs_2_.1, bf16[32,4096]{1,0:T(8,128)(2,1)} %refs_3_.1), custom_call_target="tpu_custom_call" | custom-call | tf_op jit(solution)/shard_map/pallas_call | solution.py:431
  31.7 42.0 %shard_map.68 = (bf16[256,512]{1,0:T(8,128)(2,1)}, bf16[256,512]{1,0:T(8,128)(2,1)}, bf16[256,512]{1,0:T(8,128)(2,1)}) custom-call(bf16[256,512]{1,0:T(8,128)(2,1)} %get-tuple-element.10.q_hbm, bf16[256,512]{1,0:T(8,128)(2,1)} %get-tuple-element.11.k_hbm, bf16[256,512]{1,0:T(8,128)(2,1)} %get-tuple-element.12.v_hbm, bf16[256,512]{1,0:T(8,128)(2,1)} %get-tuple-element.13.d_hbm), custom_call_target="tpu_custom_call" | custom-call | tf_op jit(solution)/shard_map/pallas_call | solution.py:339
  73.6 23.4 %shard_map.69 = (bf16[32,4096]{1,0:T(8,128)(2,1)}, bf16[32,4096]{1,0:T(8,128)(2,1)}, bf16[32,4096]{1,0:T(8,128)(2,1)}) custom-call(bf16[256,512]{1,0:T(8,128)(2,1)} %get-tuple-element.14.refs_0_, bf16[256,512]{1,0:T(8,128)(2,1)} %get-tuple-element.15.refs_1_, bf16[256,512]{1,0:T(8,128)(2,1)} %get-tuple-element.16.refs_2_), custom_call_target="tpu_custom_call" | custom-call | tf_op jit(solution)/shard_map/pallas_call | solution.py:431
  97.0 0.0 copy-start.1
  97.1 1.7 %copy.10 = bf16[32,4096]{1,0:T(8,128)(2,1)} copy(bf16[32,4096]{1,0:T(8,128)(2,1)} %get-tuple-element.20) | data formatting | bytes 524288
  98.8 0.0 copy-done.1
  98.8 0.0 copy-start
  98.8 0.7 copy.11
  99.5 0.3 copy-done
  99.8 0.7 copy.12
Async XLA Ops:
  97.0 1.7 %copy-start.1 = (bf16[32,4096]{1,0:T(8,128)(2,1)S(1)}, bf16[32,4096]{1,0:T(8,128)(2,1)}, u32[]{:S(2)}) copy-start(bf16[32,4096]{1,0:T(8,128)(2,1)} %get-tuple-element.21) | copy-start | bytes 786436
  98.8 1.0 %copy-start = (bf16[32,4096]{1,0:T(8,128)(2,1)S(1)}, bf16[32,4096]{1,0:T(8,128)(2,1)}, u32[]{:S(2)}) copy-start(bf16[32,4096]{1,0:T(8,128)(2,1)} %get-tuple-element.22) | copy-start | bytes 786436

commit v8 on v7

--- a/solution.py
+++ b/solution.py
@@ -378,12 +378,14 @@
     )(q_all, k_all, v_all, d_all)
 
 
-def exchange_kernel(count, n_arrays, src_cut, dst_cut, *refs):
+def exchange_kernel(count, n_arrays, rows, src_cut, dst_cut, *refs):
     srcs = refs[:n_arrays]
     dsts = refs[n_arrays:2 * n_arrays]
-    send_sems, recv_sems, local_sems = refs[2 * n_arrays:]
+    send_sems, recv_sems, local_sems, relay_buf, relay_sems = refs[2 * n_arrays:]
     me = lax.axis_index("head")
     place = lax.axis_index("ctx")
+    far = count // 2 if count % 2 == 0 and count >= 4 else None
+    hr = rows // 2
     barrier = pltpu.get_barrier_semaphore()
     for j in range(count):
         @pl.when(me != j)
@@ -391,52 +393,94 @@
             pl.semaphore_signal(barrier, inc=1, device_id=(place, j), device_id_type=MESH)
     pl.semaphore_wait(barrier, count - 1)
 
-    def remote(a, j, dst_index):
+    def peer(step):
+        return lax.rem(me + step, count)
+
+    def copy(src, dst, sem_send, sem_recv, j):
         return pltpu.make_async_remote_copy(
-            src_ref=src_cut(srcs[a], j), dst_ref=dst_cut(dsts[a], dst_index),
-            send_sem=send_sems.at[a, j], recv_sem=recv_sems.at[a, me],
+            src_ref=src, dst_ref=dst, send_sem=sem_send, recv_sem=sem_recv,
             device_id=(place, j), device_id_type=MESH)
 
+    def direct(a, step):
+        return copy(src_cut(srcs[a], peer(step), 0, rows), dst_cut(dsts[a], me, 0, rows),
+                    send_sems.at[a, step], recv_sems.at[a, step], peer(step))
+
+    def direct_in(a, step):
+        return copy(src_cut(srcs[a], peer(step), 0, rows),
+                    dst_cut(dsts[a], peer(count - step), 0, rows),
+                    send_sems.at[a, step], recv_sems.at[a, step], peer(step))
+
+    steps = [s for s in range(1, count) if s != far]
+    for step in steps:
+        for a in range(n_arrays):
+            direct(a, step).start()
+
+    def leg_one(a, side):
+        first_row = 0 if side == 0 else hr
+        relay = peer(1) if side == 0 else peer(count - 1)
+        return copy(src_cut(srcs[a], peer(far), first_row, hr), relay_buf.at[side, a],
+                    relay_sems.at[0, 0, side, a], relay_sems.at[1, 0, side, a], relay)
+
+    def leg_two(a, side):
+        if side == 0:
+            origin, first_row, target = peer(count - 1), 0, peer(far - 1)
+        else:
+            origin, first_row, target = peer(1), hr, peer(count - far + 1)
+        return copy(relay_buf.at[side, a], dst_cut(dsts[a], origin, first_row, hr),
+                    relay_sems.at[0, 1, side, a], relay_sems.at[1, 1, side, a], target)
+
+    def leg_two_in(a, side):
+        first_row = 0 if side == 0 else hr
+        return copy(relay_buf.at[side, a], dst_cut(dsts[a], peer(far), first_row, hr),
+                    relay_sems.at[0, 1, side, a], relay_sems.at[1, 1, side, a], peer(far))
+
+    if far is not None:
+        for a in range(n_arrays):
+            for side in range(2):
+                leg_one(a, side).start()
+
     for a in range(n_arrays):
-        local = pltpu.make_async_copy(src_cut(srcs[a], me), dst_cut(dsts[a], me), local_sems.at[a])
-        local.start()
-    for step in range(1, count):
+        pltpu.make_async_copy(src_cut(srcs[a], me, 0, rows), dst_cut(dsts[a], me, 0, rows),
+                              local_sems.at[a]).start()
+
+    if far is not None:
         for a in range(n_arrays):
-            j_dyn = lax.rem(me + step, count)
-            for j in range(count):
-                @pl.when(j_dyn == j)
-                def _():
-                    remote(a, j, me).start()
+            for side in range(2):
+                leg_one(a, side).wait_recv()
+                leg_two(a, side).start()
+
     for a in range(n_arrays):
-        pltpu.make_async_copy(src_cut(srcs[a], me), dst_cut(dsts[a], me), local_sems.at[a]).wait()
-    for a in range(n_arrays):
-        for j in range(count):
-            @pl.when(me != j)
-            def _():
-                copy = pltpu.make_async_remote_copy(
-                    src_ref=src_cut(srcs[a], j), dst_ref=dst_cut(dsts[a], j),
-                    send_sem=send_sems.at[a, j], recv_sem=recv_sems.at[a, j],
-                    device_id=(place, j), device_id_type=MESH)
-                copy.wait_send()
-                copy.wait_recv()
-
-
-def exchange(arrays, out_shape, src_cut, dst_cut, collective_id, in_space, out_space):
+        pltpu.make_async_copy(src_cut(srcs[a], me, 0, rows), dst_cut(dsts[a], me, 0, rows),
+                              local_sems.at[a]).wait()
+    for step in steps:
+        for a in range(n_arrays):
+            direct_in(a, step).wait_send()
+            direct_in(a, step).wait_recv()
+    if far is not None:
+        for a in range(n_arrays):
+            for side in range(2):
+                leg_one(a, side).wait_send()
+                leg_two(a, side).wait_send()
+                leg_two_in(a, side).wait_recv()
+
+
+def exchange(arrays, out_shape, rows, cols, src_cut, dst_cut, collective_id):
     count = lax.axis_size("head")
     if count == 1:
         return tuple(arrays)
     n_arrays = len(arrays)
-    in_spec = pl.BlockSpec(memory_space=in_space)
-    out_spec = pl.BlockSpec(memory_space=out_space)
+    anywhere = pl.BlockSpec(memory_space=pl.ANY)
     return pl.pallas_call(
-        functools.partial(exchange_kernel, count, n_arrays, src_cut, dst_cut),
+        functools.partial(exchange_kernel, count, n_arrays, rows, src_cut, dst_cut),
         out_shape=tuple(jax.ShapeDtypeStruct(out_shape, arrays[0].dtype) for _ in arrays),
-        in_specs=[in_spec] * n_arrays,
-        out_specs=tuple(out_spec for _ in arrays),
+        in_specs=[anywhere] * n_arrays,
+        out_specs=tuple(anywhere for _ in arrays),
         scratch_shapes=[
             pltpu.SemaphoreType.DMA((n_arrays, count)),
             pltpu.SemaphoreType.DMA((n_arrays, count)),
             pltpu.SemaphoreType.DMA((n_arrays,)),
+            pltpu.VMEM((2, n_arrays, rows // 2, cols), arrays[0].dtype),
+            pltpu.SemaphoreType.DMA((2, 2, 2, n_arrays)),
         ],
         compiler_params=pltpu.CompilerParams(collective_id=collective_id, has_side_effects=True,
                                              vmem_limit_bytes=VMEM_ALL),
@@ -450,11 +494,11 @@
     q_all, k_all, v_all, d_all = exchange(
         (queries, key_rows, value_rows, grad_out),
         (rows_in * count, cols),
-        lambda ref, j: ref.at[:, pl.ds(j * cols, cols)],
-        lambda ref, j: ref.at[pl.ds(j * rows_in, rows_in), :],
+        rows_in,
+        cols,
+        lambda ref, j, r0, nr: ref.at[pl.ds(r0, nr), pl.ds(j * cols, cols)],
+        lambda ref, j, r0, nr: ref.at[pl.ds(j * rows_in + r0, nr), :],
         1,
-        pl.ANY,
-        pl.ANY,
     )
     rows_here = q_all.shape[0]
     scale = (HEAD_DIM * rows_here * lax.axis_size("ctx")) ** (-0.5)
@@ -462,11 +506,11 @@
     result_q, result_k, result_v = exchange(
         (grad_q, grad_k, grad_v),
         (rows_in, width),
-        lambda ref, j: ref.at[pl.ds(j * rows_in, rows_in), :],
-        lambda ref, j: ref.at[:, pl.ds(j * cols, cols)],
+        rows_in,
+        cols,
+        lambda ref, j, r0, nr: ref.at[pl.ds(j * rows_in + r0, nr), :],
+        lambda ref, j, r0, nr: ref.at[pl.ds(r0, nr), pl.ds(j * cols, cols)],
         2,
-        pl.ANY,
-        pl.ANY,
     )
     return (result_q, result_k, result_v)
 

time: 101 us -> 103 us (1.020)
  Pallas kernels: 96.4 us -> 98.9 us
    pallas_call x1, Pallas kernels: 42 us -> 43.5 us  [core_math(): pl.pallas_call(functools.partial(core_kernel, plane, planes, rounds, half...]
where the time goes in v8:
time: 103 us
  Pallas kernels  98.9 us (96%)
  local copies, waits for them, and re-layouts  3.46 us (3%)
    pallas_call x2, Pallas kernels, exchange(): pl.pallas_call(functools.partial(exchange_kernel, count, n_arrays, rows,...  55.4 us
    pallas_call x1, Pallas kernels, core_math(): pl.pallas_call(functools.partial(core_kernel, plane, planes, rounds, half...  43.5 us
    unnamed x7, local copies, waits for them, and re-layouts  3.46 us

profile of v8, /device:TPU:1, one launch (start us, length us, event | category | flops | bytes accessed | tf_op | source)
XLA Modules:
  0.0 103.1 jit_solution(1232652405342132145)
XLA Ops:
  0.6 30.2 %shard_map.67 = (bf16[256,512]{1,0:T(8,128)(2,1)}, bf16[256,512]{1,0:T(8,128)(2,1)}, bf16[256,512]{1,0:T(8,128)(2,1)}, bf16[256,512]{1,0:T(8,128)(2,1)}) custom-call(bf16[32,4096]{1,0:T(8,128)(2,1)} %refs_0_.1, bf16[32,4096]{1,0:T(8,128)(2,1)} %refs_1_.1, bf16[32,4096]{1,0:T(8,128)(2,1)} %refs_2_.1, bf16[32,4096]{1,0:T(8,128)(2,1)} %refs_3_.1), custom_call_target="tpu_custom_call" | custom-call | tf_op jit(solution)/shard_map/pallas_call | solution.py:473
  30.9 43.5 %shard_map.68 = (bf16[256,512]{1,0:T(8,128)(2,1)}, bf16[256,512]{1,0:T(8,128)(2,1)}, bf16[256,512]{1,0:T(8,128)(2,1)}) custom-call(bf16[256,512]{1,0:T(8,128)(2,1)} %get-tuple-element.10.q_hbm, bf16[256,512]{1,0:T(8,128)(2,1)} %get-tuple-element.11.k_hbm, bf16[256,512]{1,0:T(8,128)(2,1)} %get-tuple-element.12.v_hbm, bf16[256,512]{1,0:T(8,128)(2,1)} %get-tuple-element.13.d_hbm), custom_call_target="tpu_custom_call" | custom-call | tf_op jit(solution)/shard_map/pallas_call | solution.py:339
  74.4 25.2 %shard_map.69 = (bf16[32,4096]{1,0:T(8,128)(2,1)}, bf16[32,4096]{1,0:T(8,128)(2,1)}, bf16[32,4096]{1,0:T(8,128)(2,1)}) custom-call(bf16[256,512]{1,0:T(8,128)(2,1)} %get-tuple-element.14.refs_0_, bf16[256,512]{1,0:T(8,128)(2,1)} %get-tuple-element.15.refs_1_, bf16[256,512]{1,0:T(8,128)(2,1)} %get-tuple-element.16.refs_2_), custom_call_target="tpu_custom_call" | custom-call | tf_op jit(solution)/shard_map/pallas_call | solution.py:473
  99.6 0.0 copy-start.1
  99.6 1.7 %copy.10 = bf16[32,4096]{1,0:T(8,128)(2,1)} copy(bf16[32,4096]{1,0:T(8,128)(2,1)} %get-tuple-element.20) | data formatting | bytes 524288
  101.3 0.0 copy-done.1
  101.3 0.0 copy-start
  101.3 0.7 copy.11
  102.0 0.3 copy-done
  102.4 0.7 copy.12
Async XLA Ops:
  99.6 1.7 %copy-start.1 = (bf16[32,4096]{1,0:T(8,128)(2,1)S(1)}, bf16[32,4096]{1,0:T(8,128)(2,1)}, u32[]{:S(2)}) copy-start(bf16[32,4096]{1,0:T(8,128)(2,1)} %get-tuple-element.21) | copy-start | bytes 786436
  101.3 1.0 %copy-start = (bf16[32,4096]{1,0:T(8,128)(2,1)S(1)}, bf16[32,4096]{1,0:T(8,128)(2,1)}, u32[]{:S(2)}) copy-start(bf16[32,4096]{1,0:T(8,128)(2,1)} %get-tuple-element.22) | copy-start | bytes 786436

commit v9 on v7

--- a/solution.py
+++ b/solution.py
@@ -20,13 +20,13 @@
                            precision=lax.Precision.HIGHEST if precise else None)
 
 
-def core_kernel(plane, planes, rounds, half, nblocks, heads, scale,
+def core_kernel(plane, planes, rounds, half, nblocks, heads, scale, ways,
                 q_hbm, k_hbm, v_hbm, d_hbm, gq_hbm, gk_hbm, gv_hbm,
                 q_ref, k_ref, v_ref, d_ref, gq_ref, gk_ref, gv_ref, io_sems,
                 fwd_in, bwd_in, kv_blk, g_blk, acc_q, acc_k, acc_v,
                 peer_f, peer_b, th_f, th_b, in_b1, pre, tz_f, tz_b, got_f, got_b,
                 ez_f, ez_b, out_d, in_d, res_f, res_b, fin_f, fin_b,
-                fwd_out, bwd_out, sems):
+                fwd_out, bwd_out, sems, x_sems):
     me = lax.axis_index("ctx")
     head = lax.axis_index("head")
     core = lax.rem(me, 2)
@@ -60,13 +60,50 @@
             pl.semaphore_signal(barrier, inc=1, device_id=dev(x, z - shift), device_id_type=MESH)
 
         peers = peers + (z + shift < planes).astype(jnp.int32) + (z >= shift).astype(jnp.int32)
-
-    loads = [pltpu.make_async_copy(hbm, ref, io_sems.at[i])
-             for i, (hbm, ref) in enumerate(zip((q_hbm, k_hbm, v_hbm, d_hbm), (q_ref, k_ref, v_ref, d_ref)))]
+    for j in range(ways):
+        @pl.when(head != j)
+        def _():
+            pl.semaphore_signal(barrier, inc=1, device_id=(me, j), device_id_type=MESH)
+    pl.semaphore_wait(barrier, peers + (ways - 1))
+
+    rows_in = q_hbm.shape[0]
+    cols_in = q_ref.shape[1]
+    hbm_in = (q_hbm, k_hbm, v_hbm, d_hbm)
+    vm_in = (q_ref, k_ref, v_ref, d_ref)
+
+    def spread(a, j):
+        return pltpu.make_async_remote_copy(
+            src_ref=hbm_in[a].at[:, pl.ds(j * cols_in, cols_in)],
+            dst_ref=vm_in[a].at[pl.ds(head * rows_in, rows_in)],
+            send_sem=x_sems.at[0, a, j], recv_sem=x_sems.at[1, a, head],
+            device_id=(me, j), device_id_type=MESH)
+
+    def spread_in(a, j):
+        return pltpu.make_async_remote_copy(
+            src_ref=hbm_in[a].at[:, pl.ds(j * cols_in, cols_in)],
+            dst_ref=vm_in[a].at[pl.ds(j * rows_in, rows_in)],
+            send_sem=x_sems.at[0, a, j], recv_sem=x_sems.at[1, a, j],
+            device_id=(me, j), device_id_type=MESH)
+
+    loads = [pltpu.make_async_copy(hbm_in[a].at[:, pl.ds(head * cols_in, cols_in)],
+                                   vm_in[a].at[pl.ds(head * rows_in, rows_in)], io_sems.at[a])
+             for a in range(4)]
+    for step in range(1, ways):
+        for a in range(4):
+            j_dyn = lax.rem(head + step, ways)
+            for j in range(ways):
+                @pl.when(j_dyn == j)
+                def _():
+                    spread(a, j).start()
     for copy in loads:
         copy.start()
     for copy in loads:
         copy.wait()
+    for a in range(4):
+        for j in range(ways):
+            @pl.when(head != j)
+            def _():
+                spread_in(a, j).wait_recv()
 
     blk = GROUP
     dim = HEAD_DIM
@@ -87,7 +124,6 @@
         fwd_in[rows, :] = kv_sum
         bwd_in[rows, :] = g_sum
 
-    pl.semaphore_wait(barrier, peers)
 
     def remote(src, dst, sem_send, sem_recv, device):
         return pltpu.make_async_remote_copy(
@@ -260,26 +296,50 @@
 
     for h in range(heads):
         rows = slice(h * dim, (h + 1) * dim)
-        kv_in = fwd_out[rows, :]
-        kv_states = []
+        running = fwd_out[rows, :]
         for n in range(nblocks):
-            kv_states.append(kv_in)
+            block_sum = kv_blk[n, rows, :]
+            kv_blk[n, rows, :] = running
             if n + 1 < nblocks:
-                kv_in = kv_in + kv_blk[n, rows, :]
-        g_in = bwd_out[rows, :]
-        g_states = [None] * nblocks
+                running = running + block_sum
+        running = bwd_out[rows, :]
         for n in reversed(range(nblocks)):
-            g_states[n] = g_in
+            block_sum = g_blk[n, rows, :]
+            g_blk[n, rows, :] = running
             if n > 0:
-                g_in = g_in + g_blk[n, rows, :]
-        for n in range(nblocks):
-            out_rows = slice(n * blk, (n + 1) * blk)
+                running = running + block_sum
+
+    vm_out = (gq_ref, gk_ref, gv_ref)
+    hbm_out = (gq_hbm, gk_hbm, gv_hbm)
+
+    def gather_out(a, j):
+        return pltpu.make_async_remote_copy(
+            src_ref=vm_out[a].at[pl.ds(j * rows_in, rows_in)],
+            dst_ref=hbm_out[a].at[:, pl.ds(head * cols_in, cols_in)],
+            send_sem=x_sems.at[0, 4 + a, j], recv_sem=x_sems.at[1, 4 + a, head],
+            device_id=(me, j), device_id_type=MESH)
+
+    def gather_out_in(a, j):
+        return pltpu.make_async_remote_copy(
+            src_ref=vm_out[a].at[pl.ds(j * rows_in, rows_in)],
+            dst_ref=hbm_out[a].at[:, pl.ds(j * cols_in, cols_in)],
+            send_sem=x_sems.at[0, 4 + a, j], recv_sem=x_sems.at[1, 4 + a, j],
+            device_id=(me, j), device_id_type=MESH)
+
+    stores = [pltpu.make_async_copy(vm_out[a].at[pl.ds(head * rows_in, rows_in)],
+                                    hbm_out[a].at[:, pl.ds(head * cols_in, cols_in)], io_sems.at[4 + a])
+              for a in range(3)]
+    per_block = blk // rows_in
+    for n in range(nblocks):
+        out_rows = slice(n * blk, (n + 1) * blk)
+        for h in range(heads):
+            rows = slice(h * dim, (h + 1) * dim)
             out_cols = slice(h * dim, (h + 1) * dim)
             kf = cut(k_ref, n, h).astype(jnp.float32)
             vf = cut(v_ref, n, h).astype(jnp.float32)
             df = cut(d_ref, n, h).astype(jnp.float32)
-            kv_s = kv_states[n]
-            g_s = g_states[n]
+            kv_s = kv_blk[n, rows, :]
+            g_s = g_blk[n, rows, :]
             gq_ref[out_rows, out_cols] = (
                 scale * (acc_q[out_rows, out_cols] + _dot(df, kv_s, precise=True))
             ).astype(gq_ref.dtype)
@@ -289,11 +349,16 @@
             gv_ref[out_rows, out_cols] = (
                 acc_v[out_rows, out_cols] + scale * _dot(kf, g_s, tb=True, precise=True)
             ).astype(gv_ref.dtype)
-
-    stores = [pltpu.make_async_copy(ref, hbm, io_sems.at[4 + i])
-              for i, (ref, hbm) in enumerate(zip((gq_ref, gk_ref, gv_ref), (gq_hbm, gk_hbm, gv_hbm)))]
-    for copy in stores:
-        copy.start()
+        for j in range(n * per_block, (n + 1) * per_block):
+            for a in range(3):
+                @pl.when(head != j)
+                def _():
+                    gather_out(a, j).start()
+
+                @pl.when(head == j)
+                def _():
+                    stores[a].start()
+
     for copy in first + last_pair:
         copy.wait_send()
     for s in range(2):
@@ -315,19 +380,33 @@
             down.wait_send()
     for copy in stores:
         copy.wait()
+    for a in range(4):
+        for j in range(ways):
+            @pl.when(head != j)
+            def _():
+                spread_in(a, j).wait_send()
+    for a in range(3):
+        for j in range(ways):
+            @pl.when(head != j)
+            def _():
+                gather_out_in(a, j).wait_send()
+                gather_out_in(a, j).wait_recv()
 
 
 PLANE = 4
 VMEM_ALL = 67043328
 
 
-def core_math(q_all, k_all, v_all, d_all, scale):
+def core_math(q_rows, k_rows, v_rows, d_rows):
     count = lax.axis_size("ctx")
+    ways = lax.axis_size("head")
+    rows_in, full_width = q_rows.shape
+    tokens, width = rows_in * ways, full_width // ways
+    scale = (HEAD_DIM * tokens * count) ** (-0.5)
     chips = count // 2
     plane = PLANE if chips % PLANE == 0 else 1
     planes = chips // plane
     rounds = max(1, (planes - 1).bit_length())
-    tokens, width = q_all.shape
     heads = width // HEAD_DIM
     nblocks = tokens // GROUP
     rows = heads * HEAD_DIM
@@ -337,12 +416,12 @@
     anywhere = pl.BlockSpec(memory_space=pl.ANY)
     f32 = jnp.float32
     return pl.pallas_call(
-        functools.partial(core_kernel, plane, planes, rounds, half, nblocks, heads, scale),
-        out_shape=(jax.ShapeDtypeStruct(q_all.shape, q_all.dtype),) * 3,
+        functools.partial(core_kernel, plane, planes, rounds, half, nblocks, heads, scale, ways),
+        out_shape=(jax.ShapeDtypeStruct(q_rows.shape, q_rows.dtype),) * 3,
         in_specs=[anywhere] * 4,
         out_specs=(anywhere,) * 3,
         scratch_shapes=[
-            *[pltpu.VMEM((tokens, width), q_all.dtype) for _ in range(7)],
+            *[pltpu.VMEM((tokens, width), q_rows.dtype) for _ in range(7)],
             pltpu.SemaphoreType.DMA((7,)),
             pltpu.VMEM((rows, cols), f32),
             pltpu.VMEM((rows, cols), f32),
@@ -372,10 +451,11 @@
             pltpu.VMEM((rows, cols), f32),
             pltpu.VMEM((rows, cols), f32),
             pltpu.SemaphoreType.DMA((2, 5, 2, max(plane, rounds))),
+            pltpu.SemaphoreType.DMA((2, 7, ways)),
         ],
         compiler_params=pltpu.CompilerParams(collective_id=0, has_side_effects=True,
                                              vmem_limit_bytes=VMEM_ALL),
-    )(q_all, k_all, v_all, d_all)
+    )(q_rows, k_rows, v_rows, d_rows)
 
 
 def exchange_kernel(count, n_arrays, src_cut, dst_cut, *refs):
@@ -444,31 +524,7 @@
 
 
 def per_device(queries, key_rows, value_rows, grad_out):
-    count = lax.axis_size("head")
-    rows_in, width = queries.shape
-    cols = width // count
-    q_all, k_all, v_all, d_all = exchange(
-        (queries, key_rows, value_rows, grad_out),
-        (rows_in * count, cols),
-        lambda ref, j: ref.at[:, pl.ds(j * cols, cols)],
-        lambda ref, j: ref.at[pl.ds(j * rows_in, rows_in), :],
-        1,
-        pl.ANY,
-        pl.ANY,
-    )
-    rows_here = q_all.shape[0]
-    scale = (HEAD_DIM * rows_here * lax.axis_size("ctx")) ** (-0.5)
-    grad_q, grad_k, grad_v = core_math(q_all, k_all, v_all, d_all, scale)
-    result_q, result_k, result_v = exchange(
-        (grad_q, grad_k, grad_v),
-        (rows_in, width),
-        lambda ref, j: ref.at[pl.ds(j * rows_in, rows_in), :],
-        lambda ref, j: ref.at[:, pl.ds(j * cols, cols)],
-        2,
-        pl.ANY,
-        pl.ANY,
-    )
-    return (result_q, result_k, result_v)
+    return core_math(queries, key_rows, value_rows, grad_out)
 
 
 def solution(mesh):

time: 101 us -> 91.7 us (0.908)
  Pallas kernels: 96.4 us -> 87.4 us
    pallas_call x2 -> x0, Pallas kernels: 54.4 us -> none  [exchange(): pl.pallas_call(functools.partial(exchange_kernel, count, n_arrays, src_cu...]
    pallas_call x1, Pallas kernels: 42 us -> 87.4 us  [core_math(): pl.pallas_call(functools.partial(core_kernel, plane, planes, rounds, half...]
where the time goes in v9:
time: 91.7 us; the launch traced here: 91.5 us
  Pallas kernels  87.4 us (95%)
  local copies, waits for them, and re-layouts  3.46 us (4%)
    pallas_call x1, Pallas kernels, core_math(): pl.pallas_call(functools.partial(core_kernel, plane, planes, rounds, half...  87.4 us
    unnamed x7, local copies, waits for them, and re-layouts  3.46 us

profile of v9, /device:TPU:1, one launch (start us, length us, event | category | flops | bytes accessed | tf_op | source)
XLA Modules:
  0.0 91.5 jit_solution(7991239249036961174)
XLA Ops:
  0.6 87.4 %shard_map.67 = (bf16[32,4096]{1,0:T(8,128)(2,1)}, bf16[32,4096]{1,0:T(8,128)(2,1)}, bf16[32,4096]{1,0:T(8,128)(2,1)}) custom-call(bf16[32,4096]{1,0:T(8,128)(2,1)} %q_hbm.1, bf16[32,4096]{1,0:T(8,128)(2,1)} %k_hbm.1, bf16[32,4096]{1,0:T(8,128)(2,1)} %v_hbm.1, bf16[32,4096]{1,0:T(8,128)(2,1)} %d_hbm.1), custom_call_target="tpu_custom_call" | custom-call | tf_op jit(solution)/shard_map/pallas_call | solution.py:418
  88.0 0.0 copy-start.1
  88.0 1.7 %copy.10 = bf16[32,4096]{1,0:T(8,128)(2,1)} copy(bf16[32,4096]{1,0:T(8,128)(2,1)} %get-tuple-element.6) | data formatting | bytes 524288
  89.7 0.0 copy-done.1
  89.8 0.0 copy-start
  89.8 0.7 copy.11
  90.5 0.3 copy-done
  90.8 0.7 copy.12
Async XLA Ops:
  88.0 1.7 %copy-start.1 = (bf16[32,4096]{1,0:T(8,128)(2,1)S(1)}, bf16[32,4096]{1,0:T(8,128)(2,1)}, u32[]{:S(2)}) copy-start(bf16[32,4096]{1,0:T(8,128)(2,1)} %get-tuple-element.7) | copy-start | bytes 786436
  89.8 1.0 %copy-start = (bf16[32,4096]{1,0:T(8,128)(2,1)S(1)}, bf16[32,4096]{1,0:T(8,128)(2,1)}, u32[]{:S(2)}) copy-start(bf16[32,4096]{1,0:T(8,128)(2,1)} %get-tuple-element.8) | copy-start | bytes 786436

commit v10 on v1

v10 whole, which is shorter than its diff:
```python
import functools

import jax
import jax.numpy as jnp
from jax import lax
from jax.experimental import pallas as pl
from jax.experimental.pallas import tpu as pltpu
from jax.sharding import PartitionSpec as P

HEAD_DIM = 128
GROUP = 128


MESH = pl.DeviceIdType.MESH


def _dot(a, b, ta=False, tb=False, precise=False):
    dims = (((0 if ta else 1,), (1 if tb else 0,)), ((), ()))
    return lax.dot_general(a, b, dims, preferred_element_type=jnp.float32,
                           precision=lax.Precision.HIGHEST if precise else None)


def core_kernel(plane, planes, rounds, stages, nblocks, heads, scale, ways,
                q_hbm, k_hbm, v_hbm, d_hbm, gq_hbm, gk_hbm, gv_hbm,
                q_ref, k_ref, v_ref, d_ref, gq_ref, gk_ref, gv_ref, io_sems,
                fwd_in, bwd_in, kv_blk, g_blk, acc_q, acc_k, acc_v,
                peer_f, peer_b, th_f, th_b, in_b1, pre, tz_f, tz_b, got_f, got_b,
                ez_f, ez_b, out_d, in_d, res_f, res_b, fin_f, fin_b,
                fwd_out, bwd_out, sems, x_sems):
    me = lax.axis_index("ctx")
    head = lax.axis_index("head")
    core = lax.rem(me, 2)
    chip = me // 2
    x = lax.rem(chip, plane)
    z = chip // plane
    partner = me + 1 - 2 * core
    blk = GROUP
    dim = HEAD_DIM
    hs = heads // stages
    rows_s = hs * dim
    half = rows_s // 2
    qr = half // plane
    rows_in = q_hbm.shape[0]
    cols_in = q_ref.shape[1]
    cols_s = hs * dim

    def dev(xp, zp):
        return ((zp * plane + xp) * 2 + core, head)

    barrier = pltpu.get_barrier_semaphore()
    pl.semaphore_signal(barrier, inc=1, device_id=(partner, head), device_id_type=MESH)
    peers = 1
    for xp in range(plane):
        @pl.when(x != xp)
        def _():
            pl.semaphore_signal(barrier, inc=1, device_id=dev(xp, z), device_id_type=MESH)

        peers = peers + (x != xp).astype(jnp.int32)
    for k in range(rounds):
        shift = 1 << k

        @pl.when(z + shift < planes)
        def _():
            pl.semaphore_signal(barrier, inc=1, device_id=dev(x, z + shift), device_id_type=MESH)

        @pl.when(z >= shift)
        def _():
            pl.semaphore_signal(barrier, inc=1, device_id=dev(x, z - shift), device_id_type=MESH)

        peers = peers + (z + shift < planes).astype(jnp.int32) + (z >= shift).astype(jnp.int32)
    for j in range(ways):
        @pl.when(head != j)
        def _():
            pl.semaphore_signal(barrier, inc=1, device_id=(me, j), device_id_type=MESH)
    pl.semaphore_wait(barrier, peers + (ways - 1))

    hbm_in = (q_hbm, k_hbm, v_hbm, d_hbm)
    vm_in = (q_ref, k_ref, v_ref, d_ref)
    vm_out = (gq_ref, gk_ref, gv_ref)
    hbm_out = (gq_hbm, gk_hbm, gv_hbm)

    def spread(st, a, j, slot):
        return pltpu.make_async_remote_copy(
            src_ref=hbm_in[a].at[:, pl.ds(j * cols_in + st * cols_s, cols_s)],
            dst_ref=vm_in[a].at[pl.ds(slot * rows_in, rows_in), pl.ds(st * cols_s, cols_s)],
            send_sem=x_sems.at[st, 0, a, j], recv_sem=x_sems.at[st, 1, a, slot],
            device_id=(me, j), device_id_type=MESH)

    def spread_in(st, a, j):
        return spread(st, a, j, j)

    def load(st, a):
        return pltpu.make_async_copy(
            hbm_in[a].at[:, pl.ds(head * cols_in + st * cols_s, cols_s)],
            vm_in[a].at[pl.ds(head * rows_in, rows_in), pl.ds(st * cols_s, cols_s)],
            io_sems.at[st, a])

    def gather_out(st, a, j, slot):
        return pltpu.make_async_remote_copy(
            src_ref=vm_out[a].at[pl.ds(j * rows_in, rows_in), pl.ds(st * cols_s, cols_s)],
            dst_ref=hbm_out[a].at[:, pl.ds(slot * cols_in + st * cols_s, cols_s)],
            send_sem=x_sems.at[st, 0, 4 + a, j], recv_sem=x_sems.at[st, 1, 4 + a, slot],
            device_id=(me, j), device_id_type=MESH)

    def store(st, a):
        return pltpu.make_async_copy(
            vm_out[a].at[pl.ds(head * rows_in, rows_in), pl.ds(st * cols_s, cols_s)],
            hbm_out[a].at[:, pl.ds(head * cols_in + st * cols_s, cols_s)],
            io_sems.at[st, 4 + a])

    for st in range(stages):
        for step in range(1, ways):
            for a in range(4):
                j_dyn = lax.rem(head + step, ways)
                for j in range(ways):
                    @pl.when(j_dyn == j)
                    def _():
                        spread(st, a, j, head).start()
        for a in range(4):
            load(st, a).start()

    def cut(ref, n, h):
        return ref[n * blk:(n + 1) * blk, h * dim:(h + 1) * dim]

    def remote(src, dst, sem_send, sem_recv, device):
        return pltpu.make_async_remote_copy(
            src_ref=src, dst_ref=dst, send_sem=sem_send, recv_sem=sem_recv,
            device_id=device, device_id_type=MESH)

    later = lax.broadcasted_iota(jnp.int32, (blk, blk), 0)
    earlier = lax.broadcasted_iota(jnp.int32, (blk, blk), 1)
    causal = later >= earlier
    per_block = blk // rows_in

    def stage_copies(st):
        sm = sems.at[st]
        fi, bi = fwd_in.at[st], bwd_in.at[st]
        pf, pb = peer_f.at[st], peer_b.at[st]
        first = (remote(fi, pf, sm.at[0, 0, 0, 0], sm.at[1, 0, 0, 0], (partner, head)),
                 remote(bi, pb, sm.at[0, 0, 1, 0], sm.at[1, 0, 1, 0], (partner, head)))
        halves = (th_f.at[st], th_b.at[st])
        inb = in_b1.at[st]

        def scatter(s, xp):
            return remote(halves[s].at[pl.ds(xp * qr, qr)], inb.at[s, x],
                          sm.at[0, 2, s, xp], sm.at[1, 2, s, x], dev(xp, z))

        def scatter_in(s, xp):
            return remote(halves[s].at[pl.ds(xp * qr, qr)], inb.at[s, xp],
                          sm.at[0, 2, s, xp], sm.at[1, 2, s, xp], dev(xp, z))

        def z_copies(k):
            shift = 1 << k
            up = remote(tz_f.at[st, k], got_f.at[st, k], sm.at[0, 3, 0, k], sm.at[1, 3, 0, k],
                        dev(x, z + shift))
            down = remote(tz_b.at[st, k], got_b.at[st, k], sm.at[0, 3, 1, k], sm.at[1, 3, 1, k],
                          dev(x, z - shift))
            return up, down

        od, idd = out_d.at[st], in_d.at[st]

        def gather(s, xp):
            return remote(od.at[s, xp], idd.at[s, x], sm.at[0, 4, s, xp], sm.at[1, 4, s, x], dev(xp, z))

        def gather_in(s, xp):
            return remote(od.at[s, xp], idd.at[s, xp], sm.at[0, 4, s, xp], sm.at[1, 4, s, xp], dev(xp, z))

        last_pair = (remote(res_f.at[st], fin_f.at[st], sm.at[0, 1, 0, 0], sm.at[1, 1, 0, 0], (partner, head)),
                     remote(res_b.at[st], fin_b.at[st], sm.at[0, 1, 1, 0], sm.at[1, 1, 1, 0], (partner, head)))
        return first, scatter, scatter_in, z_copies, gather, gather_in, last_pair

    for st in range(stages):
        first, scatter, scatter_in, z_copies, gather, gather_in, last_pair = stage_copies(st)
        for a in range(4):
            load(st, a).wait()
            for j in range(ways):
                @pl.when(head != j)
                def _():
                    spread_in(st, a, j).wait_recv()

        for hh in range(hs):
            h = st * hs + hh
            rows = slice(hh * dim, (hh + 1) * dim)
            for n in range(nblocks):
                kv_blk[n, h * dim:(h + 1) * dim, :] = _dot(cut(v_ref, n, h), cut(k_ref, n, h), ta=True)
                g_blk[n, h * dim:(h + 1) * dim, :] = _dot(cut(d_ref, n, h), cut(q_ref, n, h), ta=True)
            kv_sum = kv_blk[0, h * dim:(h + 1) * dim, :]
            g_sum = g_blk[0, h * dim:(h + 1) * dim, :]
            for n in range(1, nblocks):
                kv_sum = kv_sum + kv_blk[n, h * dim:(h + 1) * dim, :]
                g_sum = g_sum + g_blk[n, h * dim:(h + 1) * dim, :]
            fwd_in[st, rows, :] = kv_sum
            bwd_in[st, rows, :] = g_sum

        for copy in first:
            copy.start()

        for hh in range(hs):
            h = st * hs + hh
            for n in range(nblocks):
                qb, kb, vb, db = (cut(r, n, h) for r in (q_ref, k_ref, v_ref, d_ref))
                scores = jnp.where(causal, _dot(qb, kb, tb=True) * scale, 0.0).astype(jnp.bfloat16)
                dscores = jnp.where(causal, _dot(db, vb, tb=True), 0.0).astype(jnp.bfloat16)
                out_rows = slice(n * blk, (n + 1) * blk)
                out_cols = slice(h * dim, (h + 1) * dim)
                acc_q[out_rows, out_cols] = _dot(dscores, kb)
                acc_k[out_rows, out_cols] = _dot(dscores, qb, ta=True)
                acc_v[out_rows, out_cols] = _dot(scores, db, ta=True)

        for copy in first:
            copy.wait_recv()

        for mine in range(2):
            rows = pl.ds(mine * half, half)

            @pl.when(core == mine)
            def _():
                th_f[st] = fwd_in[st, rows, :] + peer_f[st, rows, :]
                th_b[st] = bwd_in[st, rows, :] + peer_b[st, rows, :]

        halves = (th_f.at[st], th_b.at[st])
        for s in range(2):
            for xp in range(plane):
                @pl.when(x != xp)
                def _():
                    scatter(s, xp).start()
        for s in range(2):
            in_b1[st, s, x] = halves[s][pl.ds(x * qr, qr), :]
        for s in range(2):
            for xp in range(plane):
                @pl.when(x != xp)
                def _():
                    scatter_in(s, xp).wait_recv()

        run = jnp.zeros((qr, dim), jnp.float32)
        for xp in range(plane):
            pre[st, 0, xp] = run
            run = run + in_b1[st, 0, xp]
        tz_f[st, 0] = run
        run = jnp.zeros((qr, dim), jnp.float32)
        for xp in reversed(range(plane)):
            pre[st, 1, xp] = run
            run = run + in_b1[st, 1, xp]
        tz_b[st, 0] = run

        ez_f[st] = jnp.zeros((qr, dim), jnp.float32)
        ez_b[st] = jnp.zeros((qr, dim), jnp.float32)

        for k in range(rounds):
            shift = 1 << k
            up, down = z_copies(k)
            last = k == rounds - 1

            @pl.when(z + shift < planes)
            def _():
                up.start()

            @pl.when(z >= shift)
            def _():
                down.start()

            @pl.when(z >= shift)
            def _():
                up.wait_recv()
                got = got_f[st, k]
                ez_f[st] = ez_f[st] + got
                if not last:
                    tz_f[st, k + 1] = tz_f[st, k] + got

            @pl.when(z < shift)
            def _():
                if not last:
                    tz_f[st, k + 1] = tz_f[st, k]

            @pl.when(z + shift < planes)
            def _():
                down.wait_recv()
                got = got_b[st, k]
                ez_b[st] = ez_b[st] + got
                if not last:
                    tz_b[st, k + 1] = tz_b[st, k] + got

            @pl.when(z + shift >= planes)
            def _():
                if not last:
                    tz_b[st, k + 1] = tz_b[st, k]

        zs = (ez_f, ez_b)
        for s in range(2):
            for xp in range(plane):
                out_d[st, s, xp] = zs[s][st] + pre[st, s, xp]
        for s in range(2):
            for xp in range(plane):
                @pl.when(x != xp)
                def _():
                    gather(s, xp).start()
        results = (res_f, res_b)
        for s in range(2):
            results[s][st, pl.ds(x * qr, qr), :] = out_d[st, s, x]
        for s in range(2):
            for xp in range(plane):
                @pl.when(x != xp)
                def _():
                    gather_in(s, xp).wait_recv()
                    results[s][st, xp * qr:(xp + 1) * qr, :] = in_d[st, s, xp]

        for copy in last_pair:
            copy.start()
        for copy in last_pair:
            copy.wait_recv()

        for mine in range(2):
            rows = pl.ds(mine * half, half)
            other = pl.ds((1 - mine) * half, half)

            @pl.when(core == mine)
            def _():
                if mine == 0:
                    fwd_out[st, rows, :] = res_f[st]
                    fwd_out[st, other, :] = fin_f[st]
                    bwd_out[st, rows, :] = res_b[st] + peer_b[st, rows, :]
                    bwd_out[st, other, :] = fin_b[st] + peer_b[st, other, :]
                else:
                    fwd_out[st, rows, :] = res_f[st] + peer_f[st, rows, :]
                    fwd_out[st, other, :] = fin_f[st] + peer_f[st, other, :]
                    bwd_out[st, rows, :] = res_b[st]
                    bwd_out[st, other, :] = fin_b[st]

        for hh in range(hs):
            h = st * hs + hh
            srows = slice(hh * dim, (hh + 1) * dim)
            hrows = slice(h * dim, (h + 1) * dim)
            running = fwd_out[st, srows, :]
            for n in range(nblocks):
                block_sum = kv_blk[n, hrows, :]
                kv_blk[n, hrows, :] = running
                if n + 1 < nblocks:
                    running = running + block_sum
            running = bwd_out[st, srows, :]
            for n in reversed(range(nblocks)):
                block_sum = g_blk[n, hrows, :]
                g_blk[n, hrows, :] = running
                if n > 0:
                    running = running + block_sum

        for n in range(nblocks):
            out_rows = slice(n * blk, (n + 1) * blk)
            for hh in range(hs):
                h = st * hs + hh
                hrows = slice(h * dim, (h + 1) * dim)
                out_cols = slice(h * dim, (h + 1) * dim)
                kf = cut(k_ref, n, h).astype(jnp.float32)
                vf = cut(v_ref, n, h).astype(jnp.float32)
                df = cut(d_ref, n, h).astype(jnp.float32)
                kv_s = kv_blk[n, hrows, :]
                g_s = g_blk[n, hrows, :]
                gq_ref[out_rows, out_cols] = (
                    scale * (acc_q[out_rows, out_cols] + _dot(df, kv_s, precise=True))
                ).astype(gq_ref.dtype)
                gk_ref[out_rows, out_cols] = (
                    scale * (acc_k[out_rows, out_cols] + _dot(vf, g_s, precise=True))
                ).astype(gk_ref.dtype)
                gv_ref[out_rows, out_cols] = (
                    acc_v[out_rows, out_cols] + scale * _dot(kf, g_s, tb=True, precise=True)
                ).astype(gv_ref.dtype)
            for j in range(n * per_block, (n + 1) * per_block):
                for a in range(3):
                    @pl.when(head != j)
                    def _():
                        gather_out(st, a, j, head).start()

                    @pl.when(head == j)
                    def _():
                        store(st, a).start()

    for st in range(stages):
        first, scatter, scatter_in, z_copies, gather, gather_in, last_pair = stage_copies(st)
        for copy in first + last_pair:
            copy.wait_send()
        for s in range(2):
            for xp in range(plane):
                @pl.when(x != xp)
                def _():
                    scatter(s, xp).wait_send()
                    gather(s, xp).wait_send()
        for k in range(rounds):
            shift = 1 << k
            up, down = z_copies(k)

            @pl.when(z + shift < planes)
            def _():
                up.wait_send()

            @pl.when(z >= shift)
            def _():
                down.wait_send()
        for a in range(3):
            store(st, a).wait()
        for a in range(4):
            for j in range(ways):
                @pl.when(head != j)
                def _():
                    spread_in(st, a, j).wait_send()
        for a in range(3):
            for j in range(ways):
                @pl.when(head != j)
                def _():
                    gather_out(st, a, j, j).wait_send()
                    gather_out(st, a, j, j).wait_recv()


PLANE = 4
VMEM_ALL = 67043328
STAGES = 2


def core_math(q_rows, k_rows, v_rows, d_rows):
    count = lax.axis_size("ctx")
    ways = lax.axis_size("head")
    rows_in, full_width = q_rows.shape
    tokens, width = rows_in * ways, full_width // ways
    scale = (HEAD_DIM * tokens * count) ** (-0.5)
    chips = count // 2
    plane = PLANE if chips % PLANE == 0 else 1
    planes = chips // plane
    rounds = max(1, (planes - 1).bit_length())
    heads = width // HEAD_DIM
    stages = STAGES if heads % STAGES == 0 else 1
    nblocks = tokens // GROUP
    rows = heads * HEAD_DIM
    rows_s = rows // stages
    half = rows_s // 2
    qr = half // plane
    cols = HEAD_DIM
    anywhere = pl.BlockSpec(memory_space=pl.ANY)
    f32 = jnp.float32
    return pl.pallas_call(
        functools.partial(core_kernel, plane, planes, rounds, stages, nblocks, heads, scale, ways),
        out_shape=(jax.ShapeDtypeStruct(q_rows.shape, q_rows.dtype),) * 3,
        in_specs=[anywhere] * 4,
        out_specs=(anywhere,) * 3,
        scratch_shapes=[
            *[pltpu.VMEM((tokens, width), q_rows.dtype) for _ in range(7)],
            pltpu.SemaphoreType.DMA((stages, 7)),
            pltpu.VMEM((stages, rows_s, cols), f32),
            pltpu.VMEM((stages, rows_s, cols), f32),
            pltpu.VMEM((nblocks, rows, cols), f32),
            pltpu.VMEM((nblocks, rows, cols), f32),
            pltpu.VMEM((tokens, width), f32),
            pltpu.VMEM((tokens, width), f32),
            pltpu.VMEM((tokens, width), f32),
            pltpu.VMEM((stages, rows_s, cols), f32),
            pltpu.VMEM((stages, rows_s, cols), f32),
            pltpu.VMEM((stages, half, cols), f32),
            pltpu.VMEM((stages, half, cols), f32),
            pltpu.VMEM((stages, 2, plane, qr, cols), f32),
            pltpu.VMEM((stages, 2, plane, qr, cols), f32),
            pltpu.VMEM((stages, rounds, qr, cols), f32),
            pltpu.VMEM((stages, rounds, qr, cols), f32),
            pltpu.VMEM((stages, rounds, qr, cols), f32),
            pltpu.VMEM((stages, rounds, qr, cols), f32),
            pltpu.VMEM((stages, qr, cols), f32),
            pltpu.VMEM((stages, qr, cols), f32),
            pltpu.VMEM((stages, 2, plane, qr, cols), f32),
            pltpu.VMEM((stages, 2, plane, qr, cols), f32),
            pltpu.VMEM((stages, half, cols), f32),
            pltpu.VMEM((stages, half, cols), f32),
            pltpu.VMEM((stages, half, cols), f32),
            pltpu.VMEM((stages, half, cols), f32),
            pltpu.VMEM((stages, rows_s, cols), f32),
            pltpu.VMEM((stages, rows_s, cols), f32),
            pltpu.SemaphoreType.DMA((stages, 2, 5, 2, max(plane, rounds))),
            pltpu.SemaphoreType.DMA((stages, 2, 7, ways)),
        ],
        compiler_params=pltpu.CompilerParams(collective_id=0, has_side_effects=True,
                                             vmem_limit_bytes=VMEM_ALL),
    )(q_rows, k_rows, v_rows, d_rows)


def exchange_kernel(count, n_arrays, src_cut, dst_cut, *refs):
    srcs = refs[:n_arrays]
    dsts = refs[n_arrays:2 * n_arrays]
    send_sems, recv_sems, local_sems = refs[2 * n_arrays:]
    me = lax.axis_index("head")
    place = lax.axis_index("ctx")
    barrier = pltpu.get_barrier_semaphore()
    for j in range(count):
        @pl.when(me != j)
        def _():
            pl.semaphore_signal(barrier, inc=1, device_id=(place, j), device_id_type=MESH)
    pl.semaphore_wait(barrier, count - 1)

    def remote(a, j, dst_index):
        return pltpu.make_async_remote_copy(
            src_ref=src_cut(srcs[a], j), dst_ref=dst_cut(dsts[a], dst_index),
            send_sem=send_sems.at[a, j], recv_sem=recv_sems.at[a, me],
            device_id=(place, j), device_id_type=MESH)

    for a in range(n_arrays):
        local = pltpu.make_async_copy(src_cut(srcs[a], me), dst_cut(dsts[a], me), local_sems.at[a])
        local.start()
    for step in range(1, count):
        for a in range(n_arrays):
            j_dyn = lax.rem(me + step, count)
            for j in range(count):
                @pl.when(j_dyn == j)
                def _():
                    remote(a, j, me).start()
    for a in range(n_arrays):
        pltpu.make_async_copy(src_cut(srcs[a], me), dst_cut(dsts[a], me), local_sems.at[a]).wait()
    for a in range(n_arrays):
        for j in range(count):
            @pl.when(me != j)
            def _():
                copy = pltpu.make_async_remote_copy(
                    src_ref=src_cut(srcs[a], j), dst_ref=dst_cut(dsts[a], j),
                    send_sem=send_sems.at[a, j], recv_sem=recv_sems.at[a, j],
                    device_id=(place, j), device_id_type=MESH)
                copy.wait_send()
                copy.wait_recv()


def exchange(arrays, out_shape, src_cut, dst_cut, collective_id, in_space, out_space):
    count = lax.axis_size("head")
    if count == 1:
        return tuple(arrays)
    n_arrays = len(arrays)
    in_spec = pl.BlockSpec(memory_space=in_space)
    out_spec = pl.BlockSpec(memory_space=out_space)
    return pl.pallas_call(
        functools.partial(exchange_kernel, count, n_arrays, src_cut, dst_cut),
        out_shape=tuple(jax.ShapeDtypeStruct(out_shape, arrays[0].dtype) for _ in arrays),
        in_specs=[in_spec] * n_arrays,
        out_specs=tuple(out_spec for _ in arrays),
        scratch_shapes=[
            pltpu.SemaphoreType.DMA((n_arrays, count)),
            pltpu.SemaphoreType.DMA((n_arrays, count)),
            pltpu.SemaphoreType.DMA((n_arrays,)),
        ],
        compiler_params=pltpu.CompilerParams(collective_id=collective_id, has_side_effects=True,
                                             vmem_limit_bytes=VMEM_ALL),
    )(*arrays)


def per_device(queries, key_rows, value_rows, grad_out):
    return core_math(queries, key_rows, value_rows, grad_out)


def solution(mesh):
    placed = (
        P(("ctx", "head"), None),
        P(("ctx", "head"), None),
        P(("ctx", "head"), None),
        P(("ctx", "head"), None),
    )
    return jax.shard_map(
        per_device,
        mesh=mesh,
        in_specs=placed,
        out_specs=(P(("ctx", "head"), None), P(("ctx", "head"), None), P(("ctx", "head"), None)),
        check_vma=False,
    )
```

time: 193 us -> 95.7 us (0.50)
  the two profiles are of different devices: /device:TPU:6 before, /device:TPU:1 now
where the time goes in v10:
time: 95.7 us; the launch traced here: 93.9 us
  Pallas kernels  89.8 us (94%)
  local copies, waits for them, and re-layouts  3.46 us (4%)
    pallas_call x1, Pallas kernels, core_math(): pl.pallas_call(functools.partial(core_kernel, plane, planes, rounds, stag...  89.8 us
    unnamed x7, local copies, waits for them, and re-layouts  3.46 us

profile of v10, /device:TPU:1, one launch (start us, length us, event | category | flops | bytes accessed | tf_op | source)
XLA Modules:
  0.0 93.9 jit_solution(5757142113633001836)
XLA Ops:
  0.6 89.8 %shard_map.67 = (bf16[32,4096]{1,0:T(8,128)(2,1)}, bf16[32,4096]{1,0:T(8,128)(2,1)}, bf16[32,4096]{1,0:T(8,128)(2,1)}) custom-call(bf16[32,4096]{1,0:T(8,128)(2,1)} %q_hbm.1, bf16[32,4096]{1,0:T(8,128)(2,1)} %k_hbm.1, bf16[32,4096]{1,0:T(8,128)(2,1)} %v_hbm.1, bf16[32,4096]{1,0:T(8,128)(2,1)} %d_hbm.1), custom_call_target="tpu_custom_call" | custom-call | tf_op jit(solution)/shard_map/pallas_call | solution.py:437
  90.5 0.0 copy-start.1
  90.5 1.7 %copy.10 = bf16[32,4096]{1,0:T(8,128)(2,1)} copy(bf16[32,4096]{1,0:T(8,128)(2,1)} %get-tuple-element.6) | data formatting | bytes 524288
  92.2 0.0 copy-done.1
  92.2 0.0 copy-start
  92.2 0.7 copy.11
  92.9 0.3 copy-done
  93.2 0.7 copy.12
Async XLA Ops:
  90.5 1.7 %copy-start.1 = (bf16[32,4096]{1,0:T(8,128)(2,1)S(1)}, bf16[32,4096]{1,0:T(8,128)(2,1)}, u32[]{:S(2)}) copy-start(bf16[32,4096]{1,0:T(8,128)(2,1)} %get-tuple-element.7) | copy-start | bytes 786436
  92.2 1.0 %copy-start = (bf16[32,4096]{1,0:T(8,128)(2,1)S(1)}, bf16[32,4096]{1,0:T(8,128)(2,1)}, u32[]{:S(2)}) copy-start(bf16[32,4096]{1,0:T(8,128)(2,1)} %get-tuple-element.8) | copy-start | bytes 786436

commit v11 on v9

--- a/solution.py
+++ b/solution.py
@@ -18,6 +18,12 @@
     dims = (((0 if ta else 1,), (1 if tb else 0,)), ((), ()))
     return lax.dot_general(a, b, dims, preferred_element_type=jnp.float32,
                            precision=lax.Precision.HIGHEST if precise else None)
+
+
+def _split_dot(a, b, tb=False):
+    hi = b.astype(jnp.bfloat16)
+    lo = (b - hi.astype(jnp.float32)).astype(jnp.bfloat16)
+    return _dot(a, hi, tb=tb) + _dot(a, lo, tb=tb)
 
 
 def core_kernel(plane, planes, rounds, half, nblocks, heads, scale, ways,
@@ -341,13 +347,13 @@
             kv_s = kv_blk[n, rows, :]
             g_s = g_blk[n, rows, :]
             gq_ref[out_rows, out_cols] = (
-                scale * (acc_q[out_rows, out_cols] + _dot(df, kv_s, precise=True))
+                scale * (acc_q[out_rows, out_cols] + _split_dot(cut(d_ref, n, h), kv_s))
             ).astype(gq_ref.dtype)
             gk_ref[out_rows, out_cols] = (
-                scale * (acc_k[out_rows, out_cols] + _dot(vf, g_s, precise=True))
+                scale * (acc_k[out_rows, out_cols] + _split_dot(cut(v_ref, n, h), g_s))
             ).astype(gk_ref.dtype)
             gv_ref[out_rows, out_cols] = (
-                acc_v[out_rows, out_cols] + scale * _dot(kf, g_s, tb=True, precise=True)
+                acc_v[out_rows, out_cols] + scale * _split_dot(cut(k_ref, n, h), g_s, tb=True)
             ).astype(gv_ref.dtype)
         for j in range(n * per_block, (n + 1) * per_block):
             for a in range(3):

time: 91.7 us -> 90.8 us (level)
  no operation moved by 1% of the time
where the time goes in v11:
time: 90.8 us; the launch traced here: 90.6 us
  Pallas kernels  86.5 us (95%)
  local copies, waits for them, and re-layouts  3.46 us (4%)
    pallas_call x1, Pallas kernels, core_math(): pl.pallas_call(functools.partial(core_kernel, plane, planes, rounds, half...  86.5 us
    unnamed x7, local copies, waits for them, and re-layouts  3.46 us

profile of v11, /device:TPU:1, one launch (start us, length us, event | category | flops | bytes accessed | tf_op | source)
XLA Modules:
  0.0 90.6 jit_solution(14095556882378808407)
XLA Ops:
  0.6 86.5 %shard_map.67 = (bf16[32,4096]{1,0:T(8,128)(2,1)}, bf16[32,4096]{1,0:T(8,128)(2,1)}, bf16[32,4096]{1,0:T(8,128)(2,1)}) custom-call(bf16[32,4096]{1,0:T(8,128)(2,1)} %q_hbm.1, bf16[32,4096]{1,0:T(8,128)(2,1)} %k_hbm.1, bf16[32,4096]{1,0:T(8,128)(2,1)} %v_hbm.1, bf16[32,4096]{1,0:T(8,128)(2,1)} %d_hbm.1), custom_call_target="tpu_custom_call" | custom-call | tf_op jit(solution)/shard_map/pallas_call | solution.py:424
  87.1 0.0 copy-start.1
  87.1 1.7 %copy.10 = bf16[32,4096]{1,0:T(8,128)(2,1)} copy(bf16[32,4096]{1,0:T(8,128)(2,1)} %get-tuple-element.6) | data formatting | bytes 524288
  88.8 0.0 copy-done.1
  88.8 0.0 copy-start
  88.8 0.7 copy.11
  89.5 0.3 copy-done
  89.9 0.7 copy.12
Async XLA Ops:
  87.1 1.7 %copy-start.1 = (bf16[32,4096]{1,0:T(8,128)(2,1)S(1)}, bf16[32,4096]{1,0:T(8,128)(2,1)}, u32[]{:S(2)}) copy-start(bf16[32,4096]{1,0:T(8,128)(2,1)} %get-tuple-element.7) | copy-start | bytes 786436
  88.8 1.0 %copy-start = (bf16[32,4096]{1,0:T(8,128)(2,1)S(1)}, bf16[32,4096]{1,0:T(8,128)(2,1)}, u32[]{:S(2)}) copy-start(bf16[32,4096]{1,0:T(8,128)(2,1)} %get-tuple-element.8) | copy-start | bytes 786436
